TPU v7x, 256 devices: a whole 4x4x8 slice. The times are simulated.
256 devices in a mesh: lon: 32 (over y, x, core), lat: 8 (over z).
Axes of the slice: x: 4, y: 4, z: 8, core: 2. Of those that a mesh axis runs over, the one named last changes fastest.
Arguments:
- winds: bfloat16 [2, 32, 4, 1536, 1024], P(None, None, None, 'lon', 'lat'), may hold values from -60 to 60
Outputs:
- basis: float32 [48, 2, 4, 1536, 1024], P(None, None, None, 'lon', 'lat')
All inputs are finite; a program needn't handle non-finite values.
Results may differ from a plain program's by a relative error of at most 0.0043.
Values may be sent and summed in bfloat16 or wider, within the bound.
No kernel may reach another device: no remote copies, remote signals or barrier semaphores. Data moves between devices by JAX's collectives and lax.ppermute only.
A program may use at most 128 MiB of HBM per device.

v0:
```python
import math

import jax
import jax.numpy as jnp
from jax import lax
from jax.sharding import Mesh
from jax.sharding import PartitionSpec as P

TIME = 32
TAPERS = 12
FREQS = 2
LON = ("lon_0", "lon_1", "lon_2")


def padded_2(x, sides, width):
    edges = {}
    for axis, dim in sides:
        size, length = (lax.axis_size(axis), x.shape[dim])
        up = [(i, (i + 1) % size) for i in range(size)]
        last = lax.slice_in_dim(x, length - width, length, axis=dim)
        leading = lax.slice_in_dim(x, 0, width, axis=dim)
        edges[dim] = (
            lax.ppermute(last, axis, up),
            lax.ppermute(leading, axis, [(b, a) for a, b in up]),
        )
    done = []
    for _, dim in sides:
        low, high = edges[dim]
        around = [(width, width) if d in done else (0, 0) for d in range(x.ndim)]
        x = jnp.concatenate([jnp.pad(low, around), x, jnp.pad(high, around)], axis=dim)
        done.append(dim)
    return x


def from_everyone(x, axis):
    copies = jnp.broadcast_to(x, (lax.axis_size(axis), *x.shape))
    return lax.all_to_all(copies, axis, split_axis=0, concat_axis=0, tiled=True)


def taken_together(x, axis):
    return from_everyone(x, axis).sum(axis=0)


def one_axis_at_a_time(x, axes):
    far, near = axes
    nearer = taken_together(x, near)
    return taken_together(nearer, far)


def taper_table(times, tapers, freqs):
    times_f = jnp.arange(times, dtype=jnp.float32)
    order_k = jnp.arange(tapers, dtype=jnp.float32)
    weights = math.sqrt(2.0 / (times + 1)) * jnp.sin(
        math.pi * (order_k[:, None] + 1.0) * (times_f[None, :] + 1.0) / (times + 1)
    )
    blocks = []
    for which in range(freqs):
        phases = 2.0 * math.pi * (7 + 2 * which) * times_f / times
        real_part = weights * jnp.cos(phases)[None, :]
        imag_part = -weights * jnp.sin(phases)[None, :]
        blocks.append(jnp.stack([real_part, imag_part], axis=1).reshape(2 * tapers, times))
    return jnp.concatenate(blocks, axis=0).astype(jnp.bfloat16)


def stencil(lon_pad, lat_pad, cos_lat, step_lon, step_lat):
    along_lon = (
        lon_pad[..., 2:, :].astype(jnp.float32) - lon_pad[..., :-2, :].astype(jnp.float32)
    ) / (2.0 * step_lon)
    fluxes = lat_pad.astype(jnp.float32) * cos_lat
    along_lat = (fluxes[..., 2:] - fluxes[..., :-2]) / (2.0 * step_lat)
    middle = cos_lat[1:-1]
    vorticity = ((along_lon[1] - along_lat[0]) / middle).astype(jnp.bfloat16)
    divergence = ((along_lon[0] + along_lat[1]) / middle).astype(jnp.bfloat16)
    return (vorticity, divergence)


def body(winds):
    lon_cells = winds.shape[3]
    lat_cells = winds.shape[4]
    levels = winds.shape[2]
    times = winds.shape[1]
    grid_lon = lon_cells * lax.axis_size(LON)
    grid_lat = lat_cells * lax.axis_size("lat")
    step_lon = 2.0 * math.pi / grid_lon
    step_lat = 2.6 / grid_lat
    padded = padded_2(winds, ((LON, 3), ("lat", 4)), 1)
    lon_pad = padded[..., :, 1:-1]
    lat_pad = padded[..., 1:-1, :]
    lat_index = lax.axis_index("lat") * lat_cells + jnp.arange(lat_cells + 2, dtype=jnp.int32) - 1
    lat_rows = lat_index.astype(jnp.float32)
    inside = jnp.logical_and(lat_index >= 0, lat_index < grid_lat)
    cos_plain = jnp.cos(-1.3 + (lat_rows + 0.5) * step_lat)
    cos_lat = jnp.where(inside, cos_plain, jnp.zeros_like(cos_plain))
    cos_lat = cos_lat.at[1:-1].set(cos_plain[1:-1])
    vorticity, divergence = stencil(lon_pad, lat_pad, cos_lat, step_lon, step_lat)
    table = taper_table(TIME, TAPERS, FREQS)
    vort_cols = jnp.dot(table, vorticity.reshape(times, -1), preferred_element_type=jnp.float32)
    div_cols = jnp.dot(table, divergence.reshape(times, -1), preferred_element_type=jnp.float32)
    snapshots = jnp.concatenate([vort_cols, div_cols], axis=1)
    columns = snapshots.reshape(FREQS, 2 * TAPERS, -1)
    total_rows = 2 * levels * grid_lon * grid_lat
    local_gram = (
        jnp.einsum("far,fbr->fab", columns, columns, precision=lax.Precision.HIGHEST) / total_rows
    )
    factor = jnp.linalg.cholesky(
        one_axis_at_a_time(local_gram, (("lon_0", "lon_1"), ("lon_2", "lat")))
    )
    basis = jax.scipy.linalg.solve_triangular(factor, columns, lower=True)
    return basis.reshape(2 * FREQS * TAPERS, 2, levels, lon_cells, lat_cells)


def solution(mesh):
    split = Mesh(
        mesh.devices.reshape(4, 4, 2, mesh.shape["lat"]), ("lon_0", "lon_1", "lon_2", "lat")
    )
    placed = (P(None, None, None, LON, "lat"),)
    return jax.shard_map(
        body,
        mesh=split,
        in_specs=placed,
        out_specs=P(None, None, None, LON, "lat"),
        check_vma=False,
    )
```

profile of v0, /device:TPU:1, one launch (start us, length us, event | category | flops | bytes accessed | tf_op | source)
XLA Modules:
  0.0 155.2 jit_solution(17197104372621735234)
XLA Ops:
  0.0 2.1 %fusion.16 = (bf16[2,32,4,1,128]{4,3,2,1,0:T(2,128)(2,1)S(1)}, bf16[2,32,4,1,128]{4,3,2,1,0:T(2,128)(2,1)}) fusion(bf16[2,32,4,48,128]{4,3,2,1,0:T(8,128)(2,1)} %param.3), kind=kLoop, calls=%fused_computation.56 | loop fusion | bytes 262144 | tf_op jit(solution)/shard_map/slice | solution.py:20
  2.1 3.2 %collective-permute-start = (bf16[2,32,4,1,128]{4,3,2,1,0:T(2,128)(2,1)}, bf16[2,32,4,1,128]{4,3,2,1,0:T(2,128)(2,1)S(1)}, u32[]{:S(2)}, u32[]{:S(2)}) collective-permute-start(bf16[2,32,4,1,128]{4,3,2,1,0:T(2,128)(2,1)} %get-tuple-element.20), channel_id=1, source_target_pairs={{8,0},{16,8},{24,16},{32,24},{40,32},{48,40},{56,48},{64,56},{72,6... | collective-permute-start | bytes 196616 | tf_op jit(solution)/shard_map/ppermute | solution.py:24
  5.3 7.0 %fusion.17 = (bf16[2,32,4,48,1]{4,3,2,1,0:T(8,128)(2,1)}, bf16[2,32,4,48,1]{4,3,2,1,0:T(8,128)(2,1)}) fusion(bf16[2,32,4,48,128]{4,3,2,1,0:T(8,128)(2,1)} %param.3), kind=kLoop, calls=%fused_computation.57 | loop fusion | bytes 98304 | tf_op jit(solution)/shard_map/slice | solution.py:20
  12.3 4.6 %copy.17 = bf16[2,32,4,48,1]{3,1,4,2,0:T(8,128)(2,1)} copy(bf16[2,32,4,48,1]{4,3,2,1,0:T(8,128)(2,1)} %get-tuple-element.21) | data formatting | bytes 49152
  16.9 1.0 collective-permute-start.2
  17.9 4.4 %copy.18 = bf16[2,32,4,48,1]{3,1,4,2,0:T(8,128)(2,1)} copy(bf16[2,32,4,48,1]{4,3,2,1,0:T(8,128)(2,1)} %get-tuple-element.22) | data formatting | bytes 49152
  22.3 3.9 %collective-permute-start.3 = (bf16[2,32,4,48,1]{3,1,4,2,0:T(8,128)(2,1)}, bf16[2,32,4,48,1]{3,1,4,2,0:T(8,128)(2,1)}, u32[]{:S(2)}, u32[]{:S(2)}) collective-permute-start(bf16[2,32,4,48,1]{3,1,4,2,0:T(8,128)(2,1)} %copy.18), channel_id=1, source_target_pairs={{1,0},{2,1},{3,2},{4,3},{5,4},{6,5},{7,6},{0,7},{9,8},{10,9},{11,1... | collective-permute-start | bytes 73736 | tf_op jit(solution)/shard_map/ppermute | solution.py:24
  28.2 1.4 fusion.18
  29.6 0.9 multiply_convert_fusion.3
  30.6 4.2 %copy.19 = bf16[2,32,4,48,1]{4,3,2,1,0:T(8,128)(2,1)} copy(bf16[2,32,4,48,1]{3,1,4,2,0:T(8,128)(2,1)} %collective-permute-done.2) | data formatting | bytes 49152
  34.9 4.1 %copy.20 = bf16[2,32,4,48,1]{4,3,2,1,0:T(8,128)(2,1)} copy(bf16[2,32,4,48,1]{3,1,4,2,0:T(8,128)(2,1)} %collective-permute-done.3) | data formatting | bytes 49152
  39.0 12.0 %convert_multiply_fusion = f32[2,32,4,48,130]{4,3,2,1,0:T(8,128)} fusion(bf16[2,32,4,48,1]{4,3,2,1,0:T(8,128)(2,1)} %copy.20, bf16[2,32,4,48,1]{4,3,2,1,0:T(8,128)(2,1)} %copy.19, bf16[2,32,4,1,128]{4,3,2,1,0:T(2,128)(2,1)S(1)} %collective-permute-done, bf16[2,32,4,48,128]{4,3,2,1,0:T(8,128)(2,1)S(1)} %copy-done.1, ...), kind=kLoop, calls=%fused_computation.2 | loop fusion | flops 23961600 | bytes 9716232 | tf_op jit(solution)/shard_map/mul | solution.py:69
  50.9 10.9 %fusion.4 = f32[2,32,4,48,128]{4,3,2,1,0:T(8,128)} fusion(f32[2,32,4,48,130]{4,3,2,1,0:T(8,128)} %convert_multiply_fusion), kind=kLoop, calls=%fused_computation.9 | loop fusion | flops 3145728 | bytes 18874368 | tf_op jit(solution)/shard_map/div | solution.py:70
  61.8 3.8 %subtract_multiply_fusion = f32[2,32,4,48,128]{4,3,2,1,0:T(8,128)S(1)} fusion(bf16[2,32,4,48,128]{4,3,2,1,0:T(8,128)(2,1)S(1)} %copy-done.1, bf16[2,32,4,1,128]{4,3,2,1,0:T(2,128)(2,1)S(1)} %collective-permute-done.1, bf16[2,32,4,1,128]{4,3,2,1,0:T(2,128)(2,1)S(1)} %collective-permute-done), kind=kLoop, calls=%fused_computation.12 | loop fusion | flops 15728640 | bytes 9568256 | tf_op jit(solution)/shard_map/div | solution.py:66
  65.6 2.9 %slice_subtract_fusion.1 = (f32[1,32,4,48,128]{4,3,2,1,0:T(8,128)}, f32[1,32,4,48,128]{4,3,2,1,0:T(8,128)S(1)}) fusion(f32[2,32,4,48,128]{4,3,2,1,0:T(8,128)S(1)} %copy-done.2, f32[2,32,4,48,128]{4,3,2,1,0:T(8,128)S(1)} %subtract_multiply_fusion), kind=kLoop, calls=%fused_computation.14 | loop fusion | flops 1572864 | bytes 18874368 | tf_op jit(solution)/shard_map/sub | solution.py:72
  68.5 3.4 %sub.21 = f32[32,24576]{1,0:T(8,128)} reshape(f32[1,32,4,48,128]{4,3,2,1,0:T(8,128)} %get-tuple-element.17) | data formatting | bytes 6291456 | tf_op jit(solution)/shard_map/sub | solution.py:72
  71.9 1.9 %add.85 = f32[32,24576]{1,0:T(8,128)} reshape(f32[1,32,4,48,128]{4,3,2,1,0:T(8,128)S(1)} %get-tuple-element.18) | data formatting | bytes 6291456 | tf_op jit(solution)/shard_map/add | solution.py:73
  73.8 4.9 %fusion.5 = f32[48,24576]{1,0:T(8,128)} fusion(f32[32,24576]{1,0:T(8,128)} %sub.21, f32[24576]{0:T(1024)S(1)} %bitcast.27, bf16[24,32]{1,0:T(8,128)(2,1)S(1)} %bitcast.31, bf16[24,32]{1,0:T(8,128)(2,1)S(1)} %bitcast.29), kind=kOutput, calls=%fused_computation.19 | convolution fusion | flops 77076480 | bytes 7965696 | tf_op jit(solution)/shard_map/dot_general | solution.py:97
  78.8 2.9 %fusion.6 = f32[48,24576]{1,0:T(8,128)} fusion(f32[32,24576]{1,0:T(8,128)S(1)} %copy-done.3, f32[24576]{0:T(1024)S(1)} %bitcast.28, bf16[24,32]{1,0:T(8,128)(2,1)S(1)} %bitcast.32, bf16[24,32]{1,0:T(8,128)(2,1)S(1)} %bitcast.30), kind=kOutput, calls=%fused_computation.20 | convolution fusion | flops 77076480 | bytes 7965696 | tf_op jit(solution)/shard_map/dot_general | solution.py:98
  81.7 4.4 %pad_maximum_fusion = f32[48,49152]{1,0:T(8,128)S(1)} fusion(f32[48,24576]{1,0:T(8,128)} %fusion.6, f32[48,24576]{1,0:T(8,128)} %fusion.5), kind=kLoop, calls=%fused_computation.5 | loop fusion | flops 2359296 | bytes 18874368 | tf_op jit(solution)/shard_map/concatenate | solution.py:99
  86.1 10.6 %convolution_multiply_fusion = f32[2,24,24]{2,1,0:T(8,128)S(1)} fusion(f32[2,24,49152]{2,1,0:T(8,128)S(1)} %bitcast.24), kind=kOutput, calls=%fused_computation.23 | convolution fusion | flops 679478400 | bytes 9441792 | tf_op jit(solution)/shard_map/far,fbr->fab/dot_general | solution.py:103
  96.7 0.9 reshape.330
  97.7 9.7 %all-to-all-start = ((f32[16,1,1152]{2,1,0:T(1,128)}), f32[16,1,1152]{2,1,0:T(1,128)S(1)}, u32[]{:S(2)}, u32[]{:S(2)}) async-start(f32[16,1,1152]{2,1,0:T(1,128)} %reshape.330), calls=%async_computation | async-start | bytes 147456 | tf_op jit(solution)/shard_map/all_to_all | solution.py:37
  107.4 7.2 %all-to-all-done = f32[16,1,1152]{2,1,0:T(1,128)S(1)} async-done(((f32[16,1,1152]{2,1,0:T(1,128)}), f32[16,1,1152]{2,1,0:T(1,128)S(1)}, u32[]{:S(2)}, u32[]{:S(2)}) %all-to-all-start) | async-done | bytes 73760 | tf_op jit(solution)/shard_map/all_to_all | solution.py:37
  116.2 0.9 reshape.332
  117.1 5.6 %all-to-all-start.1 = ((f32[16,1,1152]{2,1,0:T(1,128)}), f32[16,1,1152]{2,1,0:T(1,128)S(1)}, u32[]{:S(2)}, u32[]{:S(2)}) async-start(f32[16,1,1152]{2,1,0:T(1,128)} %reshape.332), calls=%async_computation.1 | async-start | bytes 147456 | tf_op jit(solution)/shard_map/all_to_all | solution.py:37
  122.7 6.6 %all-to-all-done.1 = f32[16,1,1152]{2,1,0:T(1,128)S(1)} async-done(((f32[16,1,1152]{2,1,0:T(1,128)}), f32[16,1,1152]{2,1,0:T(1,128)S(1)}, u32[]{:S(2)}, u32[]{:S(2)}) %all-to-all-start.1) | async-done | bytes 73760 | tf_op jit(solution)/shard_map/all_to_all | solution.py:37
  129.3 0.7 reduce.9
  130.4 4.4 %custom-call.8 = f32[2,24,24]{2,1,0:T(8,128)S(1)} custom-call(f32[2,24,24]{2,1,0:T(8,128)S(1)} %fusion.11), custom_call_target="Cholesky" | custom-call | tf_op jit(solution)/shard_map/jit(cholesky)/cholesky | solution.py:105
  135.0 3.7 %custom-call.9 = f32[2,1,24,24]{2,3,1,0:T(8,128)S(1)} custom-call(f32[2,1,24,24]{3,2,1,0:T(8,128)S(1)} %select_bitcast_fusion), custom_call_target="InvertDiagBlocksLowerTriangular" | custom-call | tf_op jit(solution)/shard_map/jit(_solve_triangular)/vmap()/triangular_solve | solution.py:108
  138.7 11.1 %fusion.9 = f32[2,24,49152]{2,1,0:T(8,128)S(1)} fusion(f32[2,24,49152]{2,1,0:T(8,128)} %bitcast.25, f32[2,1,24,24]{2,3,1,0:T(8,128)S(1)} %custom-call.9), kind=kOutput, calls=%fused_computation.24 | convolution fusion | flops 679477248 | bytes 18878976 | tf_op jit(solution)/shard_map/jit(_solve_triangular)/vmap()/triangular_solve | solution.py:108
  149.8 5.4 %copy.21 = f32[6,8,384,128]{3,2,1,0:T(8,128)} copy(f32[6,8,384,128]{3,1,2,0:T(8,128)S(1)} %bitcast.26) | data formatting | bytes 18874368
  (39 shorter events, 4.2 us)
Async XLA Ops:
  2.1 36.9 %collective-permute-start = (bf16[2,32,4,1,128]{4,3,2,1,0:T(2,128)(2,1)}, bf16[2,32,4,1,128]{4,3,2,1,0:T(2,128)(2,1)S(1)}, u32[]{:S(2)}, u32[]{:S(2)}) collective-permute-start(bf16[2,32,4,1,128]{4,3,2,1,0:T(2,128)(2,1)} %get-tuple-element.20), channel_id=1, source_target_pairs={{8,0},{16,8},{24,16},{32,24},{40,32},{48,40},{56,48},{64,56},{72,6... | collective-permute-start | bytes 196616 | tf_op jit(solution)/shard_map/ppermute | solution.py:24
  5.3 33.7 %collective-permute-start.1 = (bf16[2,32,4,1,128]{4,3,2,1,0:T(2,128)(2,1)S(1)}, bf16[2,32,4,1,128]{4,3,2,1,0:T(2,128)(2,1)S(1)}, u32[]{:S(2)}, u32[]{:S(2)}) collective-permute-start(bf16[2,32,4,1,128]{4,3,2,1,0:T(2,128)(2,1)S(1)} %get-tuple-element.19), channel_id=1, source_target_pairs={{0,8},{8,16},{16,24},{24,32},{32,40},{40,48},{48,56},{56,64},{64,7... | collective-permute-start | bytes 196616 | tf_op jit(solution)/shard_map/ppermute | solution.py:23
  12.3 26.7 %copy-start.1 = (bf16[2,32,4,48,128]{4,3,2,1,0:T(8,128)(2,1)S(1)}, bf16[2,32,4,48,128]{4,3,2,1,0:T(8,128)(2,1)}, u32[]{:S(2)}) copy-start(bf16[2,32,4,48,128]{4,3,2,1,0:T(8,128)(2,1)} %param.3) | copy-start | bytes 9437188
  16.9 13.7 %collective-permute-start.2 = (bf16[2,32,4,48,1]{3,1,4,2,0:T(8,128)(2,1)}, bf16[2,32,4,48,1]{3,1,4,2,0:T(8,128)(2,1)}, u32[]{:S(2)}, u32[]{:S(2)}) collective-permute-start(bf16[2,32,4,48,1]{3,1,4,2,0:T(8,128)(2,1)} %copy.17), channel_id=1, source_target_pairs={{0,1},{1,2},{2,3},{3,4},{4,5},{5,6},{6,7},{7,0},{8,9},{9,10},{10,1... | collective-permute-start | bytes 73736 | tf_op jit(solution)/shard_map/ppermute | solution.py:23
  22.3 12.5 %collective-permute-start.3 = (bf16[2,32,4,48,1]{3,1,4,2,0:T(8,128)(2,1)}, bf16[2,32,4,48,1]{3,1,4,2,0:T(8,128)(2,1)}, u32[]{:S(2)}, u32[]{:S(2)}) collective-permute-start(bf16[2,32,4,48,1]{3,1,4,2,0:T(8,128)(2,1)} %copy.18), channel_id=1, source_target_pairs={{1,0},{2,1},{3,2},{4,3},{5,4},{6,5},{7,6},{0,7},{9,8},{10,9},{11,1... | collective-permute-start | bytes 73736 | tf_op jit(solution)/shard_map/ppermute | solution.py:24
  61.8 3.8 %copy-start.2 = (f32[2,32,4,48,128]{4,3,2,1,0:T(8,128)S(1)}, f32[2,32,4,48,128]{4,3,2,1,0:T(8,128)}, u32[]{:S(2)}) copy-start(f32[2,32,4,48,128]{4,3,2,1,0:T(8,128)} %fusion.4) | copy-start | bytes 18874372
  68.5 5.3 %copy-start.4 = (f32[128]{0:T(128)S(1)}, f32[128]{0:T(128)}, u32[]{:S(2)}) copy-start(f32[128]{0:T(128)} %get-tuple-element.27) | copy-start | bytes 1540
  73.8 5.0 %copy-start.3 = (f32[32,24576]{1,0:T(8,128)S(1)}, f32[32,24576]{1,0:T(8,128)}, u32[]{:S(2)}) copy-start(f32[32,24576]{1,0:T(8,128)} %add.85) | copy-start | bytes 9437188
  86.1 10.6 %copy-start = (f32[48,49152]{1,0:T(8,128)}, f32[48,49152]{1,0:T(8,128)S(1)}, u32[]{:S(2)}) copy-start(f32[48,49152]{1,0:T(8,128)S(1)} %pad_maximum_fusion) | copy-start | bytes 28311556
  97.7 16.9 %all-to-all-start = ((f32[16,1,1152]{2,1,0:T(1,128)}), f32[16,1,1152]{2,1,0:T(1,128)S(1)}, u32[]{:S(2)}, u32[]{:S(2)}) async-start(f32[16,1,1152]{2,1,0:T(1,128)} %reshape.330), calls=%async_computation | async-start | bytes 147456 | tf_op jit(solution)/shard_map/all_to_all | solution.py:37
  117.1 12.2 %all-to-all-start.1 = ((f32[16,1,1152]{2,1,0:T(1,128)}), f32[16,1,1152]{2,1,0:T(1,128)S(1)}, u32[]{:S(2)}, u32[]{:S(2)}) async-start(f32[16,1,1152]{2,1,0:T(1,128)} %reshape.332), calls=%async_computation.1 | async-start | bytes 147456 | tf_op jit(solution)/shard_map/all_to_all | solution.py:37
where the time goes:
time: 156 us; the launch traced here: 155 us
  other arithmetic  46.7 us (30%)
  local copies, waits for them, and re-layouts  41.5 us (27%)
  matrix products  29.6 us (19%)
  starting transfers between devices  23.5 us (15%)
  waiting for transfers between devices  13.8 us (9%)
    unnamed x19, local copies, waits for them, and re-layouts  25 us
    all_to_all x2, starting transfers between devices, from_everyone(): return lax.all_to_all(copies, axis, split_axis=0, concat_axis=0, tiled=True)  15.3 us
    all_to_all x2, waiting for transfers between devices, from_everyone(): return lax.all_to_all(copies, axis, split_axis=0, concat_axis=0, tiled=True)  13.8 us
    mul x1, other arithmetic, stencil(): fluxes = lat_pad.astype(jnp.float32) * cos_lat  12 us
    another operation x1, matrix products, body(): basis = jax.scipy.linalg.solve_triangular(factor, columns, lower=True)  11.1 us
    div x1, other arithmetic, stencil(): along_lat = (fluxes[..., 2:] - fluxes[..., :-2]) / (2.0 * step_lat)  10.9 us
    dot_general x1, matrix products, body(): jnp.einsum('far,fbr->fab', columns, columns, precision=lax.Precision.HIGH...  10.6 us
    slice x2, local copies, waits for them, and re-layouts, padded_2(): last = lax.slice_in_dim(x, length - width, length, axis=dim)  9.06 us
  transfers between devices with their start and end apart: 6, of which 2 were waited for; matrix products, arithmetic and copies ran while one was open for 18% of the time, Pallas kernels for 0%

commit v1 on v0

v1 whole, which is shorter than its diff:
```python
import functools
import math

import jax
import jax.numpy as jnp
import numpy as np
from jax import lax
from jax.experimental import pallas as pl
from jax.experimental.pallas import tpu as pltpu
from jax.sharding import Mesh
from jax.sharding import PartitionSpec as P

TIME = 32
TAPERS = 12
FREQS = 2
COLS = 2 * TAPERS
LON = ("lon_0", "lon_1", "lon_2")
SUB = 8
F32 = jnp.float32
BF16 = jnp.bfloat16


def taper_table():
    t = np.arange(TIME, dtype=np.float32)
    k = np.arange(TAPERS, dtype=np.float32)
    weights = np.float32(math.sqrt(2.0 / (TIME + 1))) * np.sin(
        np.float32(math.pi)
        * (k[:, None] + np.float32(1.0))
        * (t[None, :] + np.float32(1.0))
        / np.float32(TIME + 1)
    )
    blocks = []
    for which in range(FREQS):
        phases = np.float32(2.0 * math.pi * (7 + 2 * which)) * t / np.float32(TIME)
        real_part = weights * np.cos(phases)[None, :]
        imag_part = -weights * np.sin(phases)[None, :]
        blocks.append(np.stack([real_part, imag_part], axis=1).reshape(COLS, TIME))
    return np.concatenate(blocks, axis=0).astype(jnp.bfloat16).astype(np.float32)


def iota(shape, dim):
    return lax.broadcasted_iota(jnp.int32, shape, dim)


def pack_kernel(w_ref, first_ref, last_ref, cols_ref, acc_ref):
    level = pl.program_id(0)
    comps, times, _, rows, lanes = w_ref.shape
    groups = rows // SUB
    deep = times * SUB
    pieces = []
    for c in range(comps):
        for g in range(groups):
            x = w_ref[c, :, 0, g * SUB : (g + 1) * SUB, :].astype(F32)
            pieces.append(x.reshape(deep, lanes).astype(BF16))
    t_of = iota((times, deep), 0) * SUB
    at = iota((times, deep), 1)
    pick_first = (at == t_of).astype(F32).astype(BF16)
    pick_last = (at == t_of + SUB - 1).astype(F32).astype(BF16)
    for c in range(comps):
        lo = jnp.dot(pick_first, pieces[c * groups], preferred_element_type=F32)
        hi = jnp.dot(pick_last, pieces[c * groups + groups - 1], preferred_element_type=F32)
        first_ref[c * times : (c + 1) * times, :] = lo.astype(BF16)
        last_ref[c * times : (c + 1) * times, :] = hi.astype(BF16)

    src = iota((lanes, lanes), 0)
    dst = iota((lanes, lanes), 1)
    blocks = comps * groups
    total = jnp.zeros((deep, lanes), F32)
    for b in range(blocks):
        spot = 2 * (level * blocks + b)
        hit = ((src == lanes - 1) & (dst == spot)) | ((src == 0) & (dst == spot + 1))
        total += jnp.dot(pieces[b], hit.astype(F32).astype(BF16), preferred_element_type=F32)

    @pl.when(level == 0)
    def _():
        acc_ref[...] = total

    @pl.when(level > 0)
    def _():
        acc_ref[...] += total

    @pl.when(level == pl.num_programs(0) - 1)
    def _():
        cols_ref[...] = acc_ref[...].astype(BF16)


def pack(winds):
    comps, times, levels, rows, lanes = winds.shape
    edge = jax.ShapeDtypeStruct((levels * comps * times, lanes), BF16)
    edge_spec = pl.BlockSpec((comps * times, lanes), lambda l: (l, 0))
    return pl.pallas_call(
        pack_kernel,
        grid=(levels,),
        in_specs=[pl.BlockSpec((comps, times, 1, rows, lanes), lambda l: (0, 0, l, 0, 0))],
        out_specs=[edge_spec, edge_spec, pl.BlockSpec((times * SUB, lanes), lambda l: (0, 0))],
        out_shape=[edge, edge, jax.ShapeDtypeStruct((times * SUB, lanes), BF16)],
        scratch_shapes=[pltpu.VMEM((times * SUB, lanes), F32)],
        compiler_params=pltpu.CompilerParams(vmem_limit_bytes=24 << 20),
        name="pack",
    )(winds)


def fields_kernel(
    step_lon, step_lat, w_ref, prev_ref, next_ref, left_ref, right_ref, cos_ref,
    f_ref, c_ref, prev_s, next_s, side_s, acc_ref,
):
    level = pl.program_id(0)
    comps, times, _, rows, lanes = w_ref.shape
    groups = rows // SUB
    deep = times * SUB
    blocks = comps * groups

    prev_s[...] = prev_ref[...].astype(F32)
    next_s[...] = next_ref[...].astype(F32)
    odd = iota((deep, lanes), 1) % 2 == 1
    side_s[...] = jnp.where(odd, right_ref[...].astype(F32), left_ref[...].astype(F32))

    cos_row = cos_ref[1:2, :]
    by_lon = jnp.broadcast_to(1.0 / (2.0 * step_lon) / cos_row, (rows, lanes))
    by_up = jnp.broadcast_to(cos_ref[2:3, :] / (2.0 * step_lat) / cos_row, (rows, lanes))
    by_down = jnp.broadcast_to(cos_ref[0:1, :] / (2.0 * step_lat) / cos_row, (rows, lanes))
    row = iota((rows, lanes), 0)
    lane = iota((rows, lanes), 1)

    def shifted(c, t):
        x = w_ref[c, t, 0].astype(F32)
        below = jnp.where(row == 0, prev_s[pl.ds(c * times + t, 1), :], pltpu.roll(x, 1, 0))
        above = jnp.where(row == rows - 1, next_s[pl.ds(c * times + t, 1), :], pltpu.roll(x, rows - 1, 0))
        halo = side_s[pl.ds(pl.multiple_of(t * SUB, SUB), SUB), :]
        parts = []
        for g in range(groups):
            spot = 2 * (level * blocks + c * groups + g) + 1
            parts.append(pltpu.roll(halo, lanes - spot, 1))
        halo = jnp.concatenate(parts, axis=0)
        west = pltpu.roll(jnp.where(lane == lanes - 1, halo, x), 1, 1)
        east = pltpu.roll(jnp.where(lane == 0, halo, x), lanes - 1, 1)
        return (above - below) * by_lon, east * by_up - west * by_down

    def one(t):
        u_lon, u_lat = shifted(0, t)
        v_lon, v_lat = shifted(1, t)
        return v_lon - u_lat, u_lon + v_lat

    @pl.loop(0, times // 2)
    def _(pair):
        even = one(2 * pair)
        later = one(2 * pair + 1)
        at = pl.ds(pl.multiple_of(pair * 2 * SUB, 2 * SUB), 2 * SUB)
        for s in range(2):
            for g in range(groups):
                cut = slice(g * SUB, (g + 1) * SUB)
                both = jnp.concatenate([even[s][cut], later[s][cut]], axis=0)
                f_ref[0, s, g, at, :] = both.astype(BF16)

    total = None
    for s in range(2):
        x = jnp.concatenate([f_ref[0, s, g] for g in range(groups)], axis=1)
        term = lax.dot_general(x, x, (((1,), (1,)), ((), ())), preferred_element_type=F32)
        total = term if total is None else total + term

    @pl.when(level == 0)
    def _():
        acc_ref[...] = total

    @pl.when(level > 0)
    def _():
        acc_ref[...] += total

    @pl.when(level == pl.num_programs(0) - 1)
    def _():
        same = iota((deep, deep), 0) % SUB == iota((deep, deep), 1) % SUB
        kept = jnp.where(same, acc_ref[...], 0.0)
        kept = kept.reshape(times, SUB, deep).sum(axis=1)
        fold = (iota((deep, times), 0) // SUB == iota((deep, times), 1)).astype(F32)
        cov = jnp.dot(kept, fold, precision=lax.Precision.HIGHEST, preferred_element_type=F32)
        c_ref[...] = jnp.concatenate([cov[q * SUB : (q + 1) * SUB] for q in range(times // SUB)], axis=1)


def fields(winds, prev_row, next_row, left, right, cos_rows, step_lon, step_lat):
    comps, times, levels, rows, lanes = winds.shape
    groups = rows // SUB
    deep = times * SUB
    edge_spec = pl.BlockSpec((comps * times, lanes), lambda l: (l, 0))
    side_spec = pl.BlockSpec((deep, lanes), lambda l: (0, 0))
    return pl.pallas_call(
        functools.partial(fields_kernel, step_lon, step_lat),
        grid=(levels,),
        in_specs=[
            pl.BlockSpec((comps, times, 1, rows, lanes), lambda l: (0, 0, l, 0, 0)),
            edge_spec, edge_spec, side_spec, side_spec,
            pl.BlockSpec((SUB, lanes), lambda l: (0, 0)),
        ],
        out_specs=[
            pl.BlockSpec((1, 2, groups, deep, lanes), lambda l: (l, 0, 0, 0, 0)),
            pl.BlockSpec((SUB, lanes), lambda l: (0, 0)),
        ],
        out_shape=[
            jax.ShapeDtypeStruct((levels, 2, groups, deep, lanes), BF16),
            jax.ShapeDtypeStruct((SUB, lanes), F32),
        ],
        scratch_shapes=[
            pltpu.VMEM((comps * times, lanes), F32),
            pltpu.VMEM((comps * times, lanes), F32),
            pltpu.VMEM((deep, lanes), F32),
            pltpu.VMEM((deep, deep), F32),
        ],
        compiler_params=pltpu.CompilerParams(vmem_limit_bytes=24 << 20),
        name="fields",
    )(winds, prev_row, next_row, left, right, cos_rows)


def basis_kernel(total_rows, sums_ref, table_ref, f_ref, out_ref, hi_ref, lo_ref):
    _, _, groups, deep, lanes = f_ref.shape
    times = deep // SUB
    outs = FREQS * COLS

    @pl.when((pl.program_id(0) == 0) & (pl.program_id(1) == 0))
    def _():
        half = lanes // 2
        flat = jnp.sum(sums_ref[...], axis=0)
        cov = jnp.concatenate([flat[:, q * times : (q + 1) * times] for q in range(times // SUB)], axis=0)
        table = table_ref[...]
        high = lax.Precision.HIGHEST
        left = jnp.dot(table, cov, precision=high, preferred_element_type=F32)
        gram = lax.dot_general(
            left, table, (((1,), (1,)), ((), ())), precision=high, preferred_element_type=F32
        ) / total_rows
        pad = jnp.zeros((COLS, half - COLS - times), F32)
        parts = []
        for f in range(FREQS):
            at = slice(f * COLS, (f + 1) * COLS)
            parts += [gram[at, at], table[at], pad]
        a = jnp.concatenate(parts, axis=1)
        row = iota((COLS, lanes), 0)
        lane = iota((COLS, lanes), 1)
        near = lane < half
        for j in range(COLS):
            pivot_row = a[j : j + 1, :]
            inv0 = 1.0 / pivot_row[:, j : j + 1]
            inv1 = 1.0 / pivot_row[:, half + j : half + j + 1]
            m = jnp.where(near, a[:, j : j + 1] * inv0, a[:, half + j : half + j + 1] * inv1)
            a = a - jnp.where(row > j, m, 0.0) * pivot_row
        rows = []
        for f in range(FREQS):
            d = jnp.sum(jnp.where(lane == f * half + row, a, 0.0), axis=1, keepdims=True)
            rows.append(a[:, f * half + COLS : f * half + COLS + times] / jnp.sqrt(d))
        w = jnp.concatenate(rows, axis=0)
        w_hi = w.astype(BF16)
        w_lo = (w - w_hi.astype(F32)).astype(BF16)
        spread = (iota((outs * SUB, outs), 0) // SUB == iota((outs * SUB, outs), 1)).astype(F32).astype(BF16)
        widen = (iota((times, deep), 0) == iota((times, deep), 1) // SUB).astype(F32).astype(BF16)
        same = iota((outs * SUB, deep), 0) % SUB == iota((outs * SUB, deep), 1) % SUB
        for term, ref in ((w_hi, hi_ref), (w_lo, lo_ref)):
            tall = jnp.dot(spread, term, preferred_element_type=F32).astype(BF16)
            full = jnp.dot(tall, widen, preferred_element_type=F32)
            ref[...] = jnp.where(same, full, 0.0).astype(BF16)

    for g in range(0, groups, 2):
        x = jnp.concatenate([f_ref[0, 0, g], f_ref[0, 0, g + 1]], axis=1)
        y = jnp.dot(hi_ref[...], x, preferred_element_type=F32)
        y += jnp.dot(lo_ref[...], x, preferred_element_type=F32)
        for e in range(2):
            part = y[:, e * lanes : (e + 1) * lanes].reshape(outs, SUB, lanes)
            out_ref[:, 0, 0, (g + e) * SUB : (g + e + 1) * SUB, :] = part


def basis_of(sums, table, f, total_rows):
    levels, kinds, groups, deep, lanes = f.shape
    outs = FREQS * COLS
    return pl.pallas_call(
        functools.partial(basis_kernel, total_rows),
        grid=(kinds, levels),
        in_specs=[
            pl.BlockSpec(sums.shape, lambda s, l: (0, 0, 0)),
            pl.BlockSpec(table.shape, lambda s, l: (0, 0)),
            pl.BlockSpec((1, 1, groups, deep, lanes), lambda s, l: (l, s, 0, 0, 0)),
        ],
        out_specs=pl.BlockSpec((outs, 1, 1, groups * SUB, lanes), lambda s, l: (0, s, l, 0, 0)),
        out_shape=jax.ShapeDtypeStruct((outs, kinds, levels, groups * SUB, lanes), F32),
        scratch_shapes=[
            pltpu.VMEM((outs * SUB, deep), BF16),
            pltpu.VMEM((outs * SUB, deep), BF16),
        ],
        compiler_params=pltpu.CompilerParams(vmem_limit_bytes=24 << 20),
        name="basis",
    )(sums, table, f)


def exchange(x, axes):
    copies = jnp.broadcast_to(x, (lax.axis_size(axes), *x.shape))
    return lax.all_to_all(copies, axes, split_axis=0, concat_axis=0, tiled=True)


def ring(x, axes, step):
    size = lax.axis_size(axes)
    return lax.ppermute(x, axes, [(i, (i + step) % size) for i in range(size)])


def body(winds):
    _, times, levels, lon_cells, lat_cells = winds.shape
    grid_lon = lon_cells * lax.axis_size(LON)
    grid_lat = lat_cells * lax.axis_size("lat")
    step_lon = 2.0 * math.pi / grid_lon
    step_lat = 2.6 / grid_lat
    first, last, cols = pack(winds)
    prev_row = ring(last, LON, 1)
    next_row = ring(first, LON, -1)
    left = ring(cols, "lat", 1)
    right = ring(cols, "lat", -1)
    shape = (SUB, lat_cells)
    index = lax.axis_index("lat") * lat_cells + iota(shape, 1) + iota(shape, 0) - 1
    inside = (index >= 0) & (index < grid_lat)
    cos_rows = jnp.where(inside, jnp.cos(-1.3 + (index.astype(F32) + 0.5) * step_lat), 0.0)
    f, cov = fields(winds, prev_row, next_row, left, right, cos_rows, step_lon, step_lat)
    near = exchange(cov, ("lon_2", "lat")).sum(axis=0)
    sums = exchange(near, ("lon_0", "lon_1"))
    return basis_of(sums, jnp.asarray(taper_table()), f, 2 * levels * grid_lon * grid_lat)


def solution(mesh):
    split = Mesh(
        mesh.devices.reshape(4, 4, 2, mesh.shape["lat"]), ("lon_0", "lon_1", "lon_2", "lat")
    )
    placed = (P(None, None, None, LON, "lat"),)
    return jax.shard_map(
        body,
        mesh=split,
        in_specs=placed,
        out_specs=P(None, None, None, LON, "lat"),
        check_vma=False,
    )
```

time: 156 us -> 71.3 us (0.46)
  other arithmetic: 46.7 us -> 0.07 us
  local copies, waits for them, and re-layouts: 41.5 us -> 5.47 us
  matrix products: 29.6 us -> 0 us
  Pallas kernels: 0 us -> 26.8 us
  blocking collectives: 0 us -> 26 us
  starting transfers between devices: 23.5 us -> 8.46 us
  waiting for transfers between devices: 13.8 us -> 4.14 us
    pallas_call x0 -> x3, Pallas kernels: none -> 26.8 us  [the longest x1 14.7 us: fields(): pl.pallas_call(functools.partial(fields_kernel, step_lon, step_lat), grid...]
    all_to_all x0 -> x2, blocking collectives: none -> 26 us  [exchange(): return lax.all_to_all(copies, axes, split_axis=0, concat_axis=0, tiled=True)]
    unnamed x19 -> x10, local copies, waits for them, and re-layouts: 25 us -> 5.46 us
    dot_general x3 -> x0, matrix products: 18.5 us -> none  [the longest x1 10.6 us: body(): jnp.einsum('far,fbr->fab', columns, columns, precision=lax.Precision.HIGH...]
    all_to_all x2 -> x0, starting transfers between devices: 15.3 us -> none  [from_everyone(): return lax.all_to_all(copies, axis, split_axis=0, concat_axis=0, tiled=True)]
    div x3 -> x0, other arithmetic: 14.7 us -> none  [the longest x1 10.9 us: stencil(): along_lat = (fluxes[..., 2:] - fluxes[..., :-2]) / (2.0 * step_lat)]
    all_to_all x2 -> x0, waiting for transfers between devices: 13.8 us -> none  [from_everyone(): return lax.all_to_all(copies, axis, split_axis=0, concat_axis=0, tiled=True)]
    mul x4 -> x0, other arithmetic: 12.1 us -> none  [the longest x1 12 us: stencil(): fluxes = lat_pad.astype(jnp.float32) * cos_lat]
  transfers between devices with their start and end apart: 6 -> 4, of which waited for: 2 -> 2; matrix products, arithmetic and copies ran while one was open for 18% -> 0% of each run, Pallas kernels for 0% -> 0%
where the time goes in v1:
time: 71.3 us; the launch traced here: 71 us
  Pallas kernels  26.8 us (38%)
  blocking collectives  26 us (36%)
  starting transfers between devices  8.46 us (12%)
  local copies, waits for them, and re-layouts  5.47 us (8%)
  waiting for transfers between devices  4.14 us (6%)
    all_to_all x2, blocking collectives, exchange(): return lax.all_to_all(copies, axes, split_axis=0, concat_axis=0, tiled=True)  26 us
    pallas_call x1, Pallas kernels, fields(): pl.pallas_call(functools.partial(fields_kernel, step_lon, step_lat), grid...  14.7 us
    pallas_call x1, Pallas kernels, basis_of(): pl.pallas_call(functools.partial(basis_kernel, total_rows), grid=(kinds,...  9.43 us
    ppermute x4, starting transfers between devices, ring(): return lax.ppermute(x, axes, [(i, (i + step) % size) for i in range(size)])  8.46 us
    unnamed x10, local copies, waits for them, and re-layouts  5.46 us
    ppermute x4, waiting for transfers between devices, ring(): return lax.ppermute(x, axes, [(i, (i + step) % size) for i in range(size)])  4.14 us
    pallas_call x1, Pallas kernels, pack(): pl.pallas_call(pack_kernel, grid=(levels,), in_specs=[pl.BlockSpec((comps...  2.65 us
  transfers between devices with their start and end apart: 4, of which 2 were waited for; matrix products, arithmetic and copies ran while one was open for 0% of the time, Pallas kernels for 0%

profile of v1, /device:TPU:1, one launch (start us, length us, event | category | flops | bytes accessed | tf_op | source)
XLA Modules:
  0.0 71.0 jit_solution(16261586588785465424)
XLA Ops:
  0.0 0.0 copy-start
  0.0 1.9 %copy-done = bf16[2,32,4,48,128]{4,3,2,1,0:T(8,128)(2,1)S(1)} copy-done((bf16[2,32,4,48,128]{4,3,2,1,0:T(8,128)(2,1)S(1)}, bf16[2,32,4,48,128]{4,3,2,1,0:T(8,128)(2,1)}, u32[]{:S(2)}) %copy-start) | copy-done | bytes 3145752
  1.9 0.0 copy-start.1
  1.9 0.0 copy-start.4
  1.9 2.6 %pack.1 = (bf16[256,128]{1,0:T(8,128)(2,1)}, bf16[256,128]{1,0:T(8,128)(2,1)}, bf16[256,128]{1,0:T(8,128)(2,1)S(1)}) custom-call(bf16[2,32,4,48,128]{4,3,2,1,0:T(8,128)(2,1)S(1)} %copy-done), custom_call_target="tpu_custom_call" | custom-call | tf_op jit(solution)/shard_map/pack/pallas_call | solution.py:91
  4.5 6.4 %collective-permute-start.3 = (bf16[256,128]{1,0:T(8,128)(2,1)S(1)}, bf16[256,128]{1,0:T(8,128)(2,1)S(1)}, u32[]{:S(2)}, u32[]{:S(2)}) collective-permute-start(bf16[256,128]{1,0:T(8,128)(2,1)S(1)} %get-tuple-element.12), channel_id=1, source_target_pairs={{0,7},{1,0},{2,1},{3,2},{4,3},{5,4},{6,5},{7,6},{8,15},{9,8},{10,9... | collective-permute-start | bytes 196616 | tf_op jit(solution)/shard_map/ppermute | solution.py:296
  10.9 0.0 collective-permute-start.2
  10.9 2.1 %collective-permute-start = (bf16[256,128]{1,0:T(8,128)(2,1)}, bf16[256,128]{1,0:T(8,128)(2,1)S(1)}, u32[]{:S(2)}, u32[]{:S(2)}) collective-permute-start(bf16[256,128]{1,0:T(8,128)(2,1)} %get-tuple-element.10), channel_id=1, source_target_pairs={{0,8},{8,16},{16,24},{24,32},{32,40},{40,48},{48,56},{56,64},{64,7... | collective-permute-start | bytes 196616 | tf_op jit(solution)/shard_map/ppermute | solution.py:296
  13.0 0.0 collective-permute-start.1
  13.0 0.1 cosine_select_fusion.cos_ref
  13.1 1.6 %collective-permute-done.prev_ref = bf16[256,128]{1,0:T(8,128)(2,1)S(1)} collective-permute-done((bf16[256,128]{1,0:T(8,128)(2,1)}, bf16[256,128]{1,0:T(8,128)(2,1)S(1)}, u32[]{:S(2)}, u32[]{:S(2)}) %collective-permute-start) | collective-permute-done | bytes 65568 | tf_op jit(solution)/shard_map/ppermute | solution.py:296
  14.6 2.5 %collective-permute-done.1.next_ref = bf16[256,128]{1,0:T(8,128)(2,1)S(1)} collective-permute-done((bf16[256,128]{1,0:T(8,128)(2,1)}, bf16[256,128]{1,0:T(8,128)(2,1)S(1)}, u32[]{:S(2)}, u32[]{:S(2)}) %collective-permute-start.1) | collective-permute-done | bytes 65568 | tf_op jit(solution)/shard_map/ppermute | solution.py:296
  17.2 0.0 collective-permute-done.3.right_ref
  17.2 0.0 collective-permute-done.2.left_ref
  17.2 0.0 copy-done.1
  17.2 14.7 %fields.1 = (bf16[4,2,6,256,128]{4,3,2,1,0:T(8,128)(2,1)S(1)}, f32[8,128]{1,0:T(8,128)S(1)}) custom-call(bf16[2,32,4,48,128]{4,3,2,1,0:T(8,128)(2,1)S(1)} %copy-done.1, bf16[256,128]{1,0:T(8,128)(2,1)S(1)} %collective-permute-done.prev_ref, bf16[256,128]{1,0:T(8,128)(2,1)S(1)} %collective-permute-done.1.next_ref, ...), custom_call_target="tpu_custom_call" | custom-call | tf_op jit(solution)/shard_map/fields/pallas_call | solution.py:185
  32.0 0.0 copy-start.2
  32.0 1.7 %copy-done.2 = bf16[4,2,6,256,128]{4,3,2,1,0:T(8,128)(2,1)} copy-done((bf16[4,2,6,256,128]{4,3,2,1,0:T(8,128)(2,1)}, bf16[4,2,6,256,128]{4,3,2,1,0:T(8,128)(2,1)S(1)}, u32[]{:S(2)}) %copy-start.2) | copy-done | bytes 3145752
  33.6 13.6 %all_to_all.10 = f32[16,8,128]{2,1,0:T(8,128)S(1)} all-to-all(f32[16,8,128]{2,1,0:T(8,128)S(1)} %broadcast_in_dim.11), channel_id=1, replica_groups=mesh['lon_0'=4,'lon_1'=4,'lon_2'=2,'lat'=8] {'lon_2','lat'}, dimensions={0} | all-to-all | bytes 131072 | tf_op jit(solution)/shard_map/all_to_all | solution.py:291
  47.2 12.5 %all_to_all.11.sums_ref = f32[16,8,128]{2,1,0:T(8,128)S(1)} all-to-all(f32[16,8,128]{2,1,0:T(8,128)S(1)} %broadcast_in_dim.12), channel_id=1, replica_groups=mesh['lon_0'=4,'lon_1'=4,'lon_2'=2,'lat'=8] {'lon_0','lon_1'}, dimensions={0} | all-to-all | bytes 131072 | tf_op jit(solution)/shard_map/all_to_all | solution.py:291
  59.7 0.0 copy-done.4
  59.7 0.0 copy-start.3
  59.7 1.9 %copy-done.3 = bf16[4,2,6,256,128]{4,3,2,1,0:T(8,128)(2,1)S(1)} copy-done((bf16[4,2,6,256,128]{4,3,2,1,0:T(8,128)(2,1)S(1)}, bf16[4,2,6,256,128]{4,3,2,1,0:T(8,128)(2,1)}, u32[]{:S(2)}) %copy-start.3) | copy-done | bytes 3145752
  61.6 9.4 %basis.1 = f32[48,2,4,48,128]{4,3,2,1,0:T(8,128)} custom-call(f32[16,8,128]{2,1,0:T(8,128)S(1)} %all_to_all.11.sums_ref, f32[48,32]{1,0:T(8,128)S(1)} %copy-done.4, bf16[4,2,6,256,128]{4,3,2,1,0:T(8,128)(2,1)S(1)} %copy-done.3), custom_call_target="tpu_custom_call" | custom-call | tf_op jit(solution)/shard_map/basis/pallas_call | solution.py:270
  (4 shorter events, 0.0 us)
Async XLA Ops:
  0.0 1.9 %copy-start = (bf16[2,32,4,48,128]{4,3,2,1,0:T(8,128)(2,1)S(1)}, bf16[2,32,4,48,128]{4,3,2,1,0:T(8,128)(2,1)}, u32[]{:S(2)}) copy-start(bf16[2,32,4,48,128]{4,3,2,1,0:T(8,128)(2,1)} %w_ref.3) | copy-start | bytes 9437188
  1.9 15.3 %copy-start.1 = (bf16[2,32,4,48,128]{4,3,2,1,0:T(8,128)(2,1)S(1)}, bf16[2,32,4,48,128]{4,3,2,1,0:T(8,128)(2,1)}, u32[]{:S(2)}) copy-start(bf16[2,32,4,48,128]{4,3,2,1,0:T(8,128)(2,1)} %w_ref.3) | copy-start | bytes 9437188
  1.9 57.8 %copy-start.4 = (f32[48,32]{1,0:T(8,128)S(1)}, f32[48,32]{1,0:T(8,128)}, u32[]{:S(2)}) copy-start(f32[48,32]{1,0:T(8,128)} %constant.23.clone.table_ref) | copy-start | bytes 18436
  4.5 12.7 %collective-permute-start.3 = (bf16[256,128]{1,0:T(8,128)(2,1)S(1)}, bf16[256,128]{1,0:T(8,128)(2,1)S(1)}, u32[]{:S(2)}, u32[]{:S(2)}) collective-permute-start(bf16[256,128]{1,0:T(8,128)(2,1)S(1)} %get-tuple-element.12), channel_id=1, source_target_pairs={{0,7},{1,0},{2,1},{3,2},{4,3},{5,4},{6,5},{7,6},{8,15},{9,8},{10,9... | collective-permute-start | bytes 196616 | tf_op jit(solution)/shard_map/ppermute | solution.py:296
  10.9 6.3 %collective-permute-start.2 = (bf16[256,128]{1,0:T(8,128)(2,1)S(1)}, bf16[256,128]{1,0:T(8,128)(2,1)S(1)}, u32[]{:S(2)}, u32[]{:S(2)}) collective-permute-start(bf16[256,128]{1,0:T(8,128)(2,1)S(1)} %get-tuple-element.12), channel_id=1, source_target_pairs={{0,1},{1,2},{2,3},{3,4},{4,5},{5,6},{6,7},{7,0},{8,9},{9,10},{10,1... | collective-permute-start | bytes 196616 | tf_op jit(solution)/shard_map/ppermute | solution.py:296
  10.9 3.7 %collective-permute-start = (bf16[256,128]{1,0:T(8,128)(2,1)}, bf16[256,128]{1,0:T(8,128)(2,1)S(1)}, u32[]{:S(2)}, u32[]{:S(2)}) collective-permute-start(bf16[256,128]{1,0:T(8,128)(2,1)} %get-tuple-element.10), channel_id=1, source_target_pairs={{0,8},{8,16},{16,24},{24,32},{32,40},{40,48},{48,56},{56,64},{64,7... | collective-permute-start | bytes 196616 | tf_op jit(solution)/shard_map/ppermute | solution.py:296
  13.0 4.2 %collective-permute-start.1 = (bf16[256,128]{1,0:T(8,128)(2,1)}, bf16[256,128]{1,0:T(8,128)(2,1)S(1)}, u32[]{:S(2)}, u32[]{:S(2)}) collective-permute-start(bf16[256,128]{1,0:T(8,128)(2,1)} %get-tuple-element.11), channel_id=1, source_target_pairs={{0,248},{8,0},{16,8},{24,16},{32,24},{40,32},{48,40},{56,48},{64,5... | collective-permute-start | bytes 196616 | tf_op jit(solution)/shard_map/ppermute | solution.py:296
  32.0 1.7 %copy-start.2 = (bf16[4,2,6,256,128]{4,3,2,1,0:T(8,128)(2,1)}, bf16[4,2,6,256,128]{4,3,2,1,0:T(8,128)(2,1)S(1)}, u32[]{:S(2)}) copy-start(bf16[4,2,6,256,128]{4,3,2,1,0:T(8,128)(2,1)S(1)} %get-tuple-element.14.f_ref) | copy-start | bytes 9437188
  59.7 1.9 %copy-start.3 = (bf16[4,2,6,256,128]{4,3,2,1,0:T(8,128)(2,1)S(1)}, bf16[4,2,6,256,128]{4,3,2,1,0:T(8,128)(2,1)}, u32[]{:S(2)}) copy-start(bf16[4,2,6,256,128]{4,3,2,1,0:T(8,128)(2,1)} %copy-done.2) | copy-start | bytes 9437188

commit v2 on v0

v2 whole, which is shorter than its diff:
```python
import functools
import math

import jax
import jax.numpy as jnp
import numpy as np
from jax import lax
from jax.experimental import pallas as pl
from jax.experimental.pallas import tpu as pltpu
from jax.sharding import Mesh
from jax.sharding import PartitionSpec as P

TIME = 32
TAPERS = 12
FREQS = 2
COLS = 2 * TAPERS
LON = ("lon_0", "lon_1", "lon_2")
SUB = 8
BIG = 16
F32 = jnp.float32
BF16 = jnp.bfloat16


def taper_table():
    t = np.arange(TIME, dtype=np.float32)
    k = np.arange(TAPERS, dtype=np.float32)
    weights = np.float32(math.sqrt(2.0 / (TIME + 1))) * np.sin(
        np.float32(math.pi)
        * (k[:, None] + np.float32(1.0))
        * (t[None, :] + np.float32(1.0))
        / np.float32(TIME + 1)
    )
    blocks = []
    for which in range(FREQS):
        phases = np.float32(2.0 * math.pi * (7 + 2 * which)) * t / np.float32(TIME)
        real_part = weights * np.cos(phases)[None, :]
        imag_part = -weights * np.sin(phases)[None, :]
        blocks.append(np.stack([real_part, imag_part], axis=1).reshape(COLS, TIME))
    return np.concatenate(blocks, axis=0).astype(jnp.bfloat16).astype(np.float32)


def iota(shape, dim):
    return lax.broadcasted_iota(jnp.int32, shape, dim)


def unit_columns(comps, thirds, halves):
    return comps * thirds * halves


def shift_table(lanes, units):
    table = np.zeros((units, 2 * lanes, 2 * lanes), np.float32)
    j = np.arange(lanes - 1)
    table[:, j + 1, j] = 1.0
    table[:, j, lanes + j + 1] = 1.0
    for u in range(units):
        table[u, lanes + 2 * u + 1, lanes - 1] = 1.0
        table[u, lanes + 2 * u, lanes] = 1.0
    return table.astype(jnp.bfloat16)


def pack_kernel(w_hbm, first_ref, last_ref, cols_ref, w_ref, first_s, last_s, acc_ref, sems):
    comps, times, levels, rows, lanes = w_ref.shape
    half = times // 2
    thirds = rows // BIG
    units = unit_columns(comps, thirds, 2)
    copies = [
        pltpu.make_async_copy(w_hbm.at[:, :, l], w_ref.at[:, :, l], sems.at[l]) for l in range(levels)
    ]
    for copy in copies:
        copy.start()
    deep = half * BIG
    at = iota((units * lanes, lanes), 0)
    spot = iota((units * lanes, lanes), 1)
    here = at % lanes
    want = at // lanes * 2
    hit = ((here == lanes - 1) & (spot == want)) | ((here == 0) & (spot == want + 1))
    hit = hit.astype(F32).astype(BF16)
    for l in range(levels):
        copies[l].wait()
        pieces = []
        for c in range(comps):
            for g in range(thirds):
                for h in range(2):
                    x = w_ref[c, h * half : (h + 1) * half, l, g * BIG : (g + 1) * BIG, :]
                    pieces.append(x.reshape(deep, lanes))
            for t in range(times):
                k = (l * comps + c) * times + t
                first_s[k : k + 1, :] = w_ref[c, t, l, 0:BIG, :].astype(F32)[0:1]
                last_s[k : k + 1, :] = w_ref[c, t, l, rows - BIG : rows, :].astype(F32)[BIG - 1 : BIG]
        total = jnp.dot(jnp.concatenate(pieces, axis=1), hit, preferred_element_type=F32)
        if l == 0:
            acc_ref[...] = total
        else:
            acc_ref[...] += pltpu.roll(total, 2 * units * l, 1)
    cols_ref[...] = acc_ref[...].astype(BF16)
    first_ref[...] = first_s[...].astype(BF16)
    last_ref[...] = last_s[...].astype(BF16)


def pack(winds):
    comps, times, levels, rows, lanes = winds.shape
    deep = times // 2 * BIG
    many = levels * comps * times
    edge = jax.ShapeDtypeStruct((many, lanes), BF16)
    return pl.pallas_call(
        pack_kernel,
        in_specs=[pl.BlockSpec(memory_space=pltpu.HBM)],
        out_shape=[edge, edge, jax.ShapeDtypeStruct((deep, lanes), BF16)],
        scratch_shapes=[
            pltpu.VMEM(winds.shape, BF16),
            pltpu.VMEM((many, lanes), F32),
            pltpu.VMEM((many, lanes), F32),
            pltpu.VMEM((deep, lanes), F32),
            pltpu.SemaphoreType.DMA((levels,)),
        ],
        compiler_params=pltpu.CompilerParams(vmem_limit_bytes=24 << 20),
        name="pack",
    )(pltpu.with_memory_space_constraint(winds, pltpu.HBM))


def fields_kernel(
    step_lon, step_lat, w_ref, prev_ref, next_ref, left_ref, right_ref, cos_ref, shift_ref,
    f_hbm, c_ref, prev_s, next_s, side_s, moved_s, f_ref, acc_ref, sems,
):
    comps, times, levels, rows, lanes = w_ref.shape
    groups = rows // SUB
    thirds = rows // BIG
    half = times // 2
    deep = times * SUB
    units = unit_columns(comps, thirds, 2)

    prev_s[...] = prev_ref[...].astype(F32)
    next_s[...] = next_ref[...].astype(F32)
    odd = iota(left_ref.shape, 1) % 2 == 1
    side = jnp.where(odd, right_ref[...].astype(F32), left_ref[...].astype(F32))
    for l in range(levels):
        mine = side if l == 0 else pltpu.roll(side, lanes - 2 * units * l, 1)
        side_s[l] = mine.astype(BF16)

    cos_row = cos_ref[1:2, :]
    by_lon = jnp.broadcast_to(1.0 / (2.0 * step_lon) / cos_row, (SUB, lanes))
    by_up = jnp.broadcast_to(cos_ref[2:3, :] / (2.0 * step_lat) / cos_row, (SUB, lanes))
    by_down = jnp.broadcast_to(cos_ref[0:1, :] / (2.0 * step_lat) / cos_row, (SUB, lanes))
    row = iota((SUB, lanes), 0)
    copies = [pltpu.make_async_copy(f_ref.at[l], f_hbm.at[l], sems.at[l]) for l in range(levels)]

    @pl.loop(0, levels)
    def _(l):
        edge = side_s[l]
        for h in range(2):
            for c in range(comps):
                for g in range(thirds):
                    x = w_ref[c, h * half : (h + 1) * half, l, g * BIG : (g + 1) * BIG, :]
                    x = jnp.concatenate([x.reshape(half * BIG, lanes), edge], axis=1)
                    moved_s[h, c, g] = jnp.dot(
                        x, shift_ref[(c * thirds + g) * 2 + h], preferred_element_type=F32
                    )

        def one(t):
            h = t // half
            by = {}
            for c in range(comps):
                x = w_ref[c, t, l].astype(F32)
                k = (l * comps + c) * times + t
                tiles = [x[g * SUB : (g + 1) * SUB] for g in range(groups)]
                up = [pltpu.roll(v, SUB - 1, 0) for v in tiles]
                down = [pltpu.roll(v, 1, 0) for v in tiles]
                up.append(jnp.broadcast_to(next_s[pl.ds(k, 1), :], (SUB, lanes)))
                down.append(jnp.broadcast_to(prev_s[pl.ds(k, 1), :], (SUB, lanes)))
                for g in range(groups):
                    above = jnp.where(row == SUB - 1, up[g + 1], up[g])
                    below = jnp.where(row == 0, down[g - 1], down[g])
                    at = (t % half) * BIG + g % 2 * SUB
                    east = moved_s[h, c, g // 2, at : at + SUB, :lanes]
                    west = moved_s[h, c, g // 2, at : at + SUB, lanes:]
                    by[c, g] = ((above - below) * by_lon, east * by_up - west * by_down)
            return [
                [by[1, g][0] - by[0, g][1] for g in range(groups)],
                [by[0, g][0] + by[1, g][1] for g in range(groups)],
            ]

        for pair in range(times // 2):
            even, later = one(2 * pair), one(2 * pair + 1)
            at = pair * 2 * SUB
            for s in range(2):
                for g in range(groups):
                    both = jnp.concatenate([even[s][g], later[s][g]], axis=0)
                    f_ref[l, s, g, at : at + 2 * SUB, :] = both.astype(BF16)

        total = None
        for s in range(2):
            x = jnp.concatenate([f_ref[l, s, g] for g in range(groups)], axis=1)
            term = lax.dot_general(x, x, (((1,), (1,)), ((), ())), preferred_element_type=F32)
            total = term if total is None else total + term

        @pl.when(l == 0)
        def _():
            acc_ref[...] = total

        @pl.when(l > 0)
        def _():
            acc_ref[...] += total

        pltpu.make_async_copy(f_ref.at[l], f_hbm.at[l], sems.at[l]).start()

    same = iota((deep, deep), 0) % SUB == iota((deep, deep), 1) % SUB
    kept = jnp.where(same, acc_ref[...], 0.0)
    kept = kept.reshape(times, SUB, deep).sum(axis=1)
    fold = (iota((deep, times), 0) // SUB == iota((deep, times), 1)).astype(F32)
    cov = jnp.dot(kept, fold, precision=lax.Precision.HIGHEST, preferred_element_type=F32)
    c_ref[...] = jnp.concatenate([cov[q * SUB : (q + 1) * SUB] for q in range(times // SUB)], axis=1)
    for copy in copies:
        copy.wait()


def fields(winds, prev_row, next_row, left, right, cos_rows, step_lon, step_lat):
    comps, times, levels, rows, lanes = winds.shape
    groups = rows // SUB
    thirds = rows // BIG
    deep = times * SUB
    shifts = jnp.asarray(shift_table(lanes, unit_columns(comps, thirds, 2)))
    whole = pl.BlockSpec(memory_space=pltpu.VMEM)
    f_shape = (levels, 2, groups, deep, lanes)
    return pl.pallas_call(
        functools.partial(fields_kernel, step_lon, step_lat),
        in_specs=[whole] * 7,
        out_specs=[pl.BlockSpec(memory_space=pltpu.HBM), whole],
        out_shape=[pltpu.HBM(f_shape, BF16), jax.ShapeDtypeStruct((SUB, lanes), F32)],
        scratch_shapes=[
            pltpu.VMEM(prev_row.shape, F32),
            pltpu.VMEM(prev_row.shape, F32),
            pltpu.VMEM((levels, *left.shape), BF16),
            pltpu.VMEM((2, comps, thirds, times // 2 * BIG, 2 * lanes), F32),
            pltpu.VMEM(f_shape, BF16),
            pltpu.VMEM((deep, deep), F32),
            pltpu.SemaphoreType.DMA((levels,)),
        ],
        compiler_params=pltpu.CompilerParams(vmem_limit_bytes=32 << 20),
        name="fields",
    )(winds, prev_row, next_row, left, right, cos_rows, shifts)


def basis_kernel(total_rows, sums_ref, table_ref, f_hbm, out_hbm, f_ref, out_ref, mix_ref, in_sems, out_sems):
    levels, kinds, groups, deep, lanes = f_ref.shape
    times = deep // SUB
    outs = FREQS * COLS
    for k in range(levels):
        pltpu.make_async_copy(f_hbm.at[k], f_ref.at[k], in_sems.at[k]).start()

    half = lanes // 2
    flat = jnp.sum(sums_ref[...], axis=0)
    cov = jnp.concatenate([flat[:, q * times : (q + 1) * times] for q in range(times // SUB)], axis=0)
    table = table_ref[...]
    high = lax.Precision.HIGHEST
    left = jnp.dot(table, cov, precision=high, preferred_element_type=F32)
    gram = lax.dot_general(
        left, table, (((1,), (1,)), ((), ())), precision=high, preferred_element_type=F32
    ) / total_rows
    pad = jnp.zeros((COLS, half - COLS - times), F32)
    parts = []
    for f in range(FREQS):
        at = slice(f * COLS, (f + 1) * COLS)
        parts += [gram[at, at], table[at], pad]
    a = jnp.concatenate(parts, axis=1)
    row = iota((COLS, lanes), 0)
    lane = iota((COLS, lanes), 1)
    near = lane < half
    for j in range(COLS):
        pivot_row = a[j : j + 1, :]
        inv0 = 1.0 / pivot_row[:, j : j + 1]
        inv1 = 1.0 / pivot_row[:, half + j : half + j + 1]
        m = jnp.where(near, a[:, j : j + 1] * inv0, a[:, half + j : half + j + 1] * inv1)
        a = a - jnp.where(row > j, m, 0.0) * pivot_row
    rows = []
    for f in range(FREQS):
        d = jnp.sum(jnp.where(lane == f * half + row, a, 0.0), axis=1, keepdims=True)
        rows.append(a[:, f * half + COLS : f * half + COLS + times] / jnp.sqrt(d))
    w = jnp.concatenate(rows, axis=0)
    w_hi = w.astype(BF16)
    w_lo = (w - w_hi.astype(F32)).astype(BF16)
    spread = (iota((outs * SUB, outs), 0) // SUB == iota((outs * SUB, outs), 1)).astype(F32).astype(BF16)
    widen = (iota((times, deep), 0) == iota((times, deep), 1) // SUB).astype(F32).astype(BF16)
    same = iota((outs * SUB, deep), 0) % SUB == iota((outs * SUB, deep), 1) % SUB
    for k, term in enumerate((w_hi, w_lo)):
        tall = jnp.dot(spread, term, preferred_element_type=F32).astype(BF16)
        full = jnp.dot(tall, widen, preferred_element_type=F32)
        mix_ref[:, k * deep : (k + 1) * deep] = jnp.where(same, full, 0.0).astype(BF16)

    @pl.loop(0, levels)
    def _(l):
        pltpu.make_async_copy(f_hbm.at[l], f_ref.at[l], in_sems.at[l]).wait()
        for s in range(kinds):
            for g in range(0, groups, 2):
                x = jnp.concatenate([f_ref[l, s, g], f_ref[l, s, g + 1]], axis=1)
                x = jnp.concatenate([x, x], axis=0)
                y = jnp.dot(mix_ref[...], x, preferred_element_type=F32)
                for e in range(2):
                    part = y[:, e * lanes : (e + 1) * lanes].reshape(outs, SUB, lanes)
                    out_ref[:, s, l, (g + e) * SUB : (g + e + 1) * SUB, :] = part
            pltpu.make_async_copy(out_ref.at[:, s, l], out_hbm.at[:, s, l], out_sems.at[s, l]).start()

    for l in range(levels):
        for s in range(kinds):
            pltpu.make_async_copy(out_ref.at[:, s, l], out_hbm.at[:, s, l], out_sems.at[s, l]).wait()


def basis_of(sums, table, f, total_rows):
    levels, kinds, groups, deep, lanes = f.shape
    outs = FREQS * COLS
    whole = pl.BlockSpec(memory_space=pltpu.VMEM)
    out_shape = (outs, kinds, levels, groups * SUB, lanes)
    return pl.pallas_call(
        functools.partial(basis_kernel, total_rows),
        in_specs=[whole, whole, pl.BlockSpec(memory_space=pltpu.HBM)],
        out_specs=pl.BlockSpec(memory_space=pltpu.HBM),
        out_shape=pltpu.HBM(out_shape, F32),
        scratch_shapes=[
            pltpu.VMEM(f.shape, BF16),
            pltpu.VMEM(out_shape, F32),
            pltpu.VMEM((outs * SUB, 2 * deep), BF16),
            pltpu.SemaphoreType.DMA((levels,)),
            pltpu.SemaphoreType.DMA((kinds, levels)),
        ],
        compiler_params=pltpu.CompilerParams(vmem_limit_bytes=32 << 20),
        name="basis",
    )(sums, table, f)


def exchange(x, axes):
    copies = jnp.broadcast_to(x, (lax.axis_size(axes), *x.shape))
    return lax.all_to_all(copies, axes, split_axis=0, concat_axis=0, tiled=True)


def ring(x, axes, step):
    size = lax.axis_size(axes)
    return lax.ppermute(x, axes, [(i, (i + step) % size) for i in range(size)])


def body(winds):
    _, times, levels, lon_cells, lat_cells = winds.shape
    grid_lon = lon_cells * lax.axis_size(LON)
    grid_lat = lat_cells * lax.axis_size("lat")
    step_lon = 2.0 * math.pi / grid_lon
    step_lat = 2.6 / grid_lat
    first, last, cols = pack(winds)
    prev_row = ring(last, LON, 1)
    next_row = ring(first, LON, -1)
    left = ring(cols, "lat", 1)
    right = ring(cols, "lat", -1)
    shape = (SUB, lat_cells)
    index = lax.axis_index("lat") * lat_cells + iota(shape, 1) + iota(shape, 0) - 1
    inside = (index >= 0) & (index < grid_lat)
    cos_rows = jnp.where(inside, jnp.cos(-1.3 + (index.astype(F32) + 0.5) * step_lat), 0.0)
    f, cov = fields(winds, prev_row, next_row, left, right, cos_rows, step_lon, step_lat)
    near = exchange(cov, ("lon_2", "lat")).sum(axis=0)
    sums = exchange(near, ("lon_0", "lon_1"))
    return basis_of(sums, jnp.asarray(taper_table()), f, 2 * levels * grid_lon * grid_lat)


def solution(mesh):
    split = Mesh(
        mesh.devices.reshape(4, 4, 2, mesh.shape["lat"]), ("lon_0", "lon_1", "lon_2", "lat")
    )
    placed = (P(None, None, None, LON, "lat"),)
    return jax.shard_map(
        body,
        mesh=split,
        in_specs=placed,
        out_specs=P(None, None, None, LON, "lat"),
        check_vma=False,
    )
```

time: 156 us -> 59.9 us (0.38)
  other arithmetic: 46.7 us -> 0.07 us
  local copies, waits for them, and re-layouts: 41.5 us -> 3.32 us
  matrix products: 29.6 us -> 0 us
  blocking collectives: 0 us -> 26.1 us
  Pallas kernels: 0 us -> 17.7 us
  starting transfers between devices: 23.5 us -> 8.54 us
  waiting for transfers between devices: 13.8 us -> 3.93 us
    all_to_all x0 -> x2, blocking collectives: none -> 26.1 us  [exchange(): return lax.all_to_all(copies, axes, split_axis=0, concat_axis=0, tiled=True)]
    unnamed x19 -> x8, local copies, waits for them, and re-layouts: 25 us -> 3.3 us
    dot_general x3 -> x0, matrix products: 18.5 us -> none  [the longest x1 10.6 us: body(): jnp.einsum('far,fbr->fab', columns, columns, precision=lax.Precision.HIGH...]
    pallas_call x0 -> x3, Pallas kernels: none -> 17.7 us  [the longest x1 7.7 us: basis_of(): pl.pallas_call(functools.partial(basis_kernel, total_rows), in_specs=[who...]
    all_to_all x2 -> x0, starting transfers between devices: 15.3 us -> none  [from_everyone(): return lax.all_to_all(copies, axis, split_axis=0, concat_axis=0, tiled=True)]
    div x3 -> x0, other arithmetic: 14.7 us -> none  [the longest x1 10.9 us: stencil(): along_lat = (fluxes[..., 2:] - fluxes[..., :-2]) / (2.0 * step_lat)]
    all_to_all x2 -> x0, waiting for transfers between devices: 13.8 us -> none  [from_everyone(): return lax.all_to_all(copies, axis, split_axis=0, concat_axis=0, tiled=True)]
    mul x4 -> x0, other arithmetic: 12.1 us -> none  [the longest x1 12 us: stencil(): fluxes = lat_pad.astype(jnp.float32) * cos_lat]
  transfers between devices with their start and end apart: 6 -> 4, of which waited for: 2 -> 2; matrix products, arithmetic and copies ran while one was open for 18% -> 0% of each run, Pallas kernels for 0% -> 0%
where the time goes in v2:
time: 59.9 us; the launch traced here: 59.7 us
  blocking collectives  26.1 us (44%)
  Pallas kernels  17.7 us (30%)
  starting transfers between devices  8.54 us (14%)
  waiting for transfers between devices  3.93 us (7%)
  local copies, waits for them, and re-layouts  3.32 us (6%)
    all_to_all x2, blocking collectives, exchange(): return lax.all_to_all(copies, axes, split_axis=0, concat_axis=0, tiled=True)  26.1 us
    ppermute x4, starting transfers between devices, ring(): return lax.ppermute(x, axes, [(i, (i + step) % size) for i in range(size)])  8.54 us
    pallas_call x1, Pallas kernels, basis_of(): pl.pallas_call(functools.partial(basis_kernel, total_rows), in_specs=[who...  7.7 us
    pallas_call x1, Pallas kernels, fields(): pl.pallas_call(functools.partial(fields_kernel, step_lon, step_lat), in_s...  6.4 us
    ppermute x4, waiting for transfers between devices, ring(): return lax.ppermute(x, axes, [(i, (i + step) % size) for i in range(size)])  3.93 us
    pallas_call x1, Pallas kernels, pack(): pl.pallas_call(pack_kernel, in_specs=[pl.BlockSpec(memory_space=pltpu.HBM...  3.64 us
    unnamed x8, local copies, waits for them, and re-layouts  3.3 us
  transfers between devices with their start and end apart: 4, of which 2 were waited for; matrix products, arithmetic and copies ran while one was open for 0% of the time, Pallas kernels for 0%

profile of v2, /device:TPU:1, one launch (start us, length us, event | category | flops | bytes accessed | tf_op | source)
XLA Modules:
  0.0 59.7 jit_solution(12892640522904750919)
XLA Ops:
  0.0 0.0 copy-start
  0.0 3.6 %pack.1 = (bf16[256,128]{1,0:T(8,128)(2,1)S(1)}, bf16[256,128]{1,0:T(8,128)(2,1)}, bf16[256,128]{1,0:T(8,128)(2,1)S(1)}) custom-call(bf16[2,32,4,48,128]{4,3,2,1,0:T(8,128)(2,1)} %w_ref.1), custom_call_target="tpu_custom_call" | custom-call | tf_op jit(solution)/shard_map/pack/pallas_call | solution.py:105
  3.7 6.5 %collective-permute-start.3 = (bf16[256,128]{1,0:T(8,128)(2,1)S(1)}, bf16[256,128]{1,0:T(8,128)(2,1)S(1)}, u32[]{:S(2)}, u32[]{:S(2)}) collective-permute-start(bf16[256,128]{1,0:T(8,128)(2,1)S(1)} %get-tuple-element.12), channel_id=1, source_target_pairs={{0,7},{1,0},{2,1},{3,2},{4,3},{5,4},{6,5},{7,6},{8,15},{9,8},{10,9... | collective-permute-start | bytes 196616 | tf_op jit(solution)/shard_map/ppermute | solution.py:336
  10.1 0.0 collective-permute-start.2
  10.1 2.0 %collective-permute-start = (bf16[256,128]{1,0:T(8,128)(2,1)}, bf16[256,128]{1,0:T(8,128)(2,1)S(1)}, u32[]{:S(2)}, u32[]{:S(2)}) collective-permute-start(bf16[256,128]{1,0:T(8,128)(2,1)} %get-tuple-element.10), channel_id=1, source_target_pairs={{0,8},{8,16},{16,24},{24,32},{32,40},{40,48},{48,56},{56,64},{64,7... | collective-permute-start | bytes 196616 | tf_op jit(solution)/shard_map/ppermute | solution.py:336
  12.2 0.0 collective-permute-start.1
  12.2 0.1 cosine_select_fusion.cos_ref
  12.3 1.6 %collective-permute-done.prev_ref = bf16[256,128]{1,0:T(8,128)(2,1)S(1)} collective-permute-done((bf16[256,128]{1,0:T(8,128)(2,1)}, bf16[256,128]{1,0:T(8,128)(2,1)S(1)}, u32[]{:S(2)}, u32[]{:S(2)}) %collective-permute-start) | collective-permute-done | bytes 65568 | tf_op jit(solution)/shard_map/ppermute | solution.py:336
  13.8 2.3 %collective-permute-done.1.next_ref = bf16[256,128]{1,0:T(8,128)(2,1)S(1)} collective-permute-done((bf16[256,128]{1,0:T(8,128)(2,1)S(1)}, bf16[256,128]{1,0:T(8,128)(2,1)S(1)}, u32[]{:S(2)}, u32[]{:S(2)}) %collective-permute-start.1) | collective-permute-done | bytes 65568 | tf_op jit(solution)/shard_map/ppermute | solution.py:336
  16.2 0.0 collective-permute-done.3.right_ref
  16.2 0.0 collective-permute-done.2.left_ref
  16.2 0.0 copy-done
  16.2 0.0 copy-start.2
  16.2 1.4 %copy-done.2 = bf16[12,256,256]{2,1,0:T(8,128)(2,1)S(1)} copy-done((bf16[12,256,256]{2,1,0:T(8,128)(2,1)S(1)}, bf16[12,256,256]{2,1,0:T(8,128)(2,1)}, u32[]{:S(2)}) %copy-start.2) | copy-done | bytes 1572888
  17.6 0.0 copy-start.3
  17.6 6.4 %fields.1 = (bf16[4,2,6,256,128]{4,3,2,1,0:T(8,128)(2,1)}, f32[8,128]{1,0:T(8,128)S(1)}) custom-call(bf16[2,32,4,48,128]{4,3,2,1,0:T(8,128)(2,1)S(1)} %copy-done, bf16[256,128]{1,0:T(8,128)(2,1)S(1)} %collective-permute-done.prev_ref, bf16[256,128]{1,0:T(8,128)(2,1)S(1)} %collective-permute-done.1.next_ref, ...), custom_call_target="tpu_custom_call" | custom-call | tf_op jit(solution)/shard_map/fields/pallas_call | solution.py:224
  24.0 13.8 %all_to_all.10 = f32[16,8,128]{2,1,0:T(8,128)S(1)} all-to-all(f32[16,8,128]{2,1,0:T(8,128)S(1)} %broadcast_in_dim.11), channel_id=1, replica_groups=mesh['lon_0'=4,'lon_1'=4,'lon_2'=2,'lat'=8] {'lon_2','lat'}, dimensions={0} | all-to-all | bytes 131072 | tf_op jit(solution)/shard_map/all_to_all | solution.py:331
  37.8 12.3 %all_to_all.11.sums_ref = f32[16,8,128]{2,1,0:T(8,128)S(1)} all-to-all(f32[16,8,128]{2,1,0:T(8,128)S(1)} %broadcast_in_dim.12), channel_id=1, replica_groups=mesh['lon_0'=4,'lon_1'=4,'lon_2'=2,'lat'=8] {'lon_0','lon_1'}, dimensions={0} | all-to-all | bytes 131072 | tf_op jit(solution)/shard_map/all_to_all | solution.py:331
  50.1 0.0 copy-done.3
  50.1 0.0 copy-start.1
  50.1 1.9 %copy-done.1 = bf16[4,2,6,256,128]{4,3,2,1,0:T(8,128)(2,1)S(1)} copy-done((bf16[4,2,6,256,128]{4,3,2,1,0:T(8,128)(2,1)S(1)}, bf16[4,2,6,256,128]{4,3,2,1,0:T(8,128)(2,1)}, u32[]{:S(2)}) %copy-start.1) | copy-done | bytes 3145752
  52.0 7.7 %basis.1 = f32[48,2,4,48,128]{4,3,2,1,0:T(8,128)} custom-call(f32[16,8,128]{2,1,0:T(8,128)S(1)} %all_to_all.11.sums_ref, f32[48,32]{1,0:T(8,128)S(1)} %copy-done.3, bf16[4,2,6,256,128]{4,3,2,1,0:T(8,128)(2,1)S(1)} %copy-done.1), custom_call_target="tpu_custom_call" | custom-call | tf_op jit(solution)/shard_map/basis/pallas_call | solution.py:312
  (4 shorter events, 0.0 us)
Async XLA Ops:
  0.0 16.2 %copy-start = (bf16[2,32,4,48,128]{4,3,2,1,0:T(8,128)(2,1)S(1)}, bf16[2,32,4,48,128]{4,3,2,1,0:T(8,128)(2,1)}, u32[]{:S(2)}) copy-start(bf16[2,32,4,48,128]{4,3,2,1,0:T(8,128)(2,1)} %w_ref.1) | copy-start | bytes 9437188
  3.7 12.5 %collective-permute-start.3 = (bf16[256,128]{1,0:T(8,128)(2,1)S(1)}, bf16[256,128]{1,0:T(8,128)(2,1)S(1)}, u32[]{:S(2)}, u32[]{:S(2)}) collective-permute-start(bf16[256,128]{1,0:T(8,128)(2,1)S(1)} %get-tuple-element.12), channel_id=1, source_target_pairs={{0,7},{1,0},{2,1},{3,2},{4,3},{5,4},{6,5},{7,6},{8,15},{9,8},{10,9... | collective-permute-start | bytes 196616 | tf_op jit(solution)/shard_map/ppermute | solution.py:336
  10.1 6.0 %collective-permute-start.2 = (bf16[256,128]{1,0:T(8,128)(2,1)S(1)}, bf16[256,128]{1,0:T(8,128)(2,1)S(1)}, u32[]{:S(2)}, u32[]{:S(2)}) collective-permute-start(bf16[256,128]{1,0:T(8,128)(2,1)S(1)} %get-tuple-element.12), channel_id=1, source_target_pairs={{0,1},{1,2},{2,3},{3,4},{4,5},{5,6},{6,7},{7,0},{8,9},{9,10},{10,1... | collective-permute-start | bytes 196616 | tf_op jit(solution)/shard_map/ppermute | solution.py:336
  10.1 3.7 %collective-permute-start = (bf16[256,128]{1,0:T(8,128)(2,1)}, bf16[256,128]{1,0:T(8,128)(2,1)S(1)}, u32[]{:S(2)}, u32[]{:S(2)}) collective-permute-start(bf16[256,128]{1,0:T(8,128)(2,1)} %get-tuple-element.10), channel_id=1, source_target_pairs={{0,8},{8,16},{16,24},{24,32},{32,40},{40,48},{48,56},{56,64},{64,7... | collective-permute-start | bytes 196616 | tf_op jit(solution)/shard_map/ppermute | solution.py:336
  12.2 4.0 %collective-permute-start.1 = (bf16[256,128]{1,0:T(8,128)(2,1)S(1)}, bf16[256,128]{1,0:T(8,128)(2,1)S(1)}, u32[]{:S(2)}, u32[]{:S(2)}) collective-permute-start(bf16[256,128]{1,0:T(8,128)(2,1)S(1)} %get-tuple-element.11), channel_id=1, source_target_pairs={{0,248},{8,0},{16,8},{24,16},{32,24},{40,32},{48,40},{56,48},{64,5... | collective-permute-start | bytes 196616 | tf_op jit(solution)/shard_map/ppermute | solution.py:336
  16.2 1.4 %copy-start.2 = (bf16[12,256,256]{2,1,0:T(8,128)(2,1)S(1)}, bf16[12,256,256]{2,1,0:T(8,128)(2,1)}, u32[]{:S(2)}) copy-start(bf16[12,256,256]{2,1,0:T(8,128)(2,1)} %constant.25.clone.shift_ref) | copy-start | bytes 4718596
  17.6 32.5 %copy-start.3 = (f32[48,32]{1,0:T(8,128)S(1)}, f32[48,32]{1,0:T(8,128)}, u32[]{:S(2)}) copy-start(f32[48,32]{1,0:T(8,128)} %constant.26.clone.table_ref) | copy-start | bytes 18436
  50.1 1.9 %copy-start.1 = (bf16[4,2,6,256,128]{4,3,2,1,0:T(8,128)(2,1)S(1)}, bf16[4,2,6,256,128]{4,3,2,1,0:T(8,128)(2,1)}, u32[]{:S(2)}) copy-start(bf16[4,2,6,256,128]{4,3,2,1,0:T(8,128)(2,1)} %get-tuple-element.14.f_hbm) | copy-start | bytes 9437188

commit v3 on v2

v3 whole, which is shorter than its diff:
```python
import functools
import math

import jax
import jax.numpy as jnp
import numpy as np
from jax import lax
from jax.experimental import pallas as pl
from jax.experimental.pallas import tpu as pltpu
from jax.sharding import Mesh
from jax.sharding import PartitionSpec as P

TIME = 32
TAPERS = 12
FREQS = 2
COLS = 2 * TAPERS
LON = ("lon_0", "lon_1", "lon_2")
SUB = 8
BIG = 16
F32 = jnp.float32
BF16 = jnp.bfloat16


def taper_table():
    t = np.arange(TIME, dtype=np.float32)
    k = np.arange(TAPERS, dtype=np.float32)
    weights = np.float32(math.sqrt(2.0 / (TIME + 1))) * np.sin(
        np.float32(math.pi)
        * (k[:, None] + np.float32(1.0))
        * (t[None, :] + np.float32(1.0))
        / np.float32(TIME + 1)
    )
    blocks = []
    for which in range(FREQS):
        phases = np.float32(2.0 * math.pi * (7 + 2 * which)) * t / np.float32(TIME)
        real_part = weights * np.cos(phases)[None, :]
        imag_part = -weights * np.sin(phases)[None, :]
        blocks.append(np.stack([real_part, imag_part], axis=1).reshape(COLS, TIME))
    return np.concatenate(blocks, axis=0).astype(jnp.bfloat16).astype(np.float32)


def iota(shape, dim):
    return lax.broadcasted_iota(jnp.int32, shape, dim)


def parity(axis):
    return lax.axis_index(axis) % 2


def as_bf16(mask):
    return mask.astype(F32).astype(BF16)


def three_terms(x):
    first = x.astype(BF16)
    rest = x - first.astype(F32)
    second = rest.astype(BF16)
    third = (rest - second.astype(F32)).astype(BF16)
    return first, second, third


def unit_of(c, g, h, thirds):
    return (c * thirds + g) * 2 + h


def pack_kernel(
    w_hbm, near_ref, far_ref, cols_ref, w_ref, first_s, last_s, acc_ref, sems,
):
    comps, times, levels, rows, lanes = w_ref.shape
    half = times // 2
    thirds = rows // BIG
    units = comps * thirds * 2
    copies = [
        pltpu.make_async_copy(w_hbm.at[:, :, l], w_ref.at[:, :, l], sems.at[l]) for l in range(levels)
    ]
    for copy in copies:
        copy.start()
    deep = half * BIG
    at = iota((units * lanes, lanes), 0)
    spot = iota((units * lanes, lanes), 1)
    here = at % lanes
    want = at // lanes * 2
    hit = as_bf16(((here == lanes - 1) & (spot == want)) | ((here == 0) & (spot == want + 1)))
    for l in range(levels):
        copies[l].wait()
        pieces = []
        for c in range(comps):
            for g in range(thirds):
                for h in range(2):
                    x = w_ref[c, h * half : (h + 1) * half, l, g * BIG : (g + 1) * BIG, :]
                    pieces.append(x.reshape(deep, lanes))
            for t in range(times):
                k = (l * comps + c) * times + t
                first_s[k : k + 1, :] = w_ref[c, t, l, 0:BIG, :].astype(F32)[0:1]
                last_s[k : k + 1, :] = w_ref[c, t, l, rows - BIG : rows, :].astype(F32)[BIG - 1 : BIG]
        total = jnp.dot(jnp.concatenate(pieces, axis=1), hit, preferred_element_type=F32)
        if l == 0:
            acc_ref[...] = total
        else:
            acc_ref[...] += pltpu.roll(total, 2 * units * l, 1)
    cols_ref[...] = acc_ref[...].astype(BF16)
    even = parity("lon_2") == 0
    near_ref[...] = jnp.where(even, last_s[...], first_s[...]).astype(BF16)
    far_ref[...] = jnp.where(even, first_s[...], last_s[...]).astype(BF16)


def pack(winds):
    comps, times, levels, rows, lanes = winds.shape
    deep = times // 2 * BIG
    many = levels * comps * times
    edge = jax.ShapeDtypeStruct((many, lanes), BF16)
    return pl.pallas_call(
        pack_kernel,
        in_specs=[pl.BlockSpec(memory_space=pltpu.HBM)],
        out_shape=[
            edge, edge, jax.ShapeDtypeStruct((deep, lanes), BF16), pltpu.VMEM(winds.shape, BF16),
        ],
        scratch_shapes=[
            pltpu.VMEM((many, lanes), F32),
            pltpu.VMEM((many, lanes), F32),
            pltpu.VMEM((deep, lanes), F32),
            pltpu.SemaphoreType.DMA((levels,)),
        ],
        compiler_params=pltpu.CompilerParams(vmem_limit_bytes=16 << 20),
        name="pack",
    )(pltpu.with_memory_space_constraint(winds, pltpu.HBM))


def factors(cos_ref, step_lon, step_lat, shape):
    cos_row = cos_ref[1:2, :]
    by_lon = jnp.broadcast_to(1.0 / (2.0 * step_lon) / cos_row, shape)
    by_up = jnp.broadcast_to(cos_ref[2:3, :] / (2.0 * step_lat) / cos_row, shape)
    by_down = jnp.broadcast_to(cos_ref[0:1, :] / (2.0 * step_lat) / cos_row, shape)
    return by_lon, by_up, by_down


def inner_kernel(step_lon, step_lat, w_ref, cos_ref, g_ref, pick_ref, moved_s):
    comps, times, levels, rows, lanes = w_ref.shape
    groups = rows // SUB
    thirds = rows // BIG
    half = times // 2
    by_lon, by_up, by_down = factors(cos_ref, step_lon, step_lat, (SUB, lanes))
    row = iota((SUB, lanes), 0)
    src = iota((lanes, lanes), 0)
    dst = iota((lanes, lanes), 1)
    shift = jnp.concatenate([as_bf16(src == dst + 1), as_bf16(src == dst - 1)], axis=1)

    wide = pick_ref.shape[1]
    src = iota((lanes, wide), 0)
    dst = iota((lanes, wide), 1)
    at = dst % lanes
    left = dst // lanes * 2
    pick_ref[...] = as_bf16(((at == 0) & (src == left)) | ((at == lanes - 1) & (src == left + 1)))

    @pl.loop(0, levels)
    def _(l):
        for h in range(2):
            for c in range(comps):
                for g in range(thirds):
                    x = w_ref[c, h * half : (h + 1) * half, l, g * BIG : (g + 1) * BIG, :]
                    moved_s[h, c, g] = jnp.dot(
                        x.reshape(half * BIG, lanes), shift, preferred_element_type=F32
                    )
        for t in range(times):
            h = t // half
            by = {}
            for c in range(comps):
                x = w_ref[c, t, l].astype(F32)
                tiles = [x[g * SUB : (g + 1) * SUB] for g in range(groups)]
                up = [pltpu.roll(v, SUB - 1, 0) for v in tiles] + [0.0]
                down = [pltpu.roll(v, 1, 0) for v in tiles] + [0.0]
                for g in range(groups):
                    above = jnp.where(row == SUB - 1, up[g + 1], up[g])
                    below = jnp.where(row == 0, down[g - 1], down[g])
                    at = (t % half) * BIG + g % 2 * SUB
                    east = moved_s[h, c, g // 2, at : at + SUB, :lanes]
                    west = moved_s[h, c, g // 2, at : at + SUB, lanes:]
                    by[c, g] = ((above - below) * by_lon, east * by_up - west * by_down)
            cut = slice(t * SUB, (t + 1) * SUB)
            for g in range(groups):
                g_ref[l, 0, g, cut, :] = by[1, g][0] - by[0, g][1]
                g_ref[l, 1, g, cut, :] = by[0, g][0] + by[1, g][1]


def inner(winds, cos_rows, step_lon, step_lat):
    comps, times, levels, rows, lanes = winds.shape
    groups = rows // SUB
    thirds = rows // BIG
    deep = times * SUB
    whole = pl.BlockSpec(memory_space=pltpu.VMEM)
    elements = winds.size
    return pl.pallas_call(
        functools.partial(inner_kernel, step_lon, step_lat),
        in_specs=[whole] * 2,
        out_specs=[whole] * 2,
        out_shape=[
            jax.ShapeDtypeStruct((levels, 2, groups, deep, lanes), F32),
            jax.ShapeDtypeStruct((lanes, comps * thirds * 2 * lanes), BF16),
        ],
        scratch_shapes=[pltpu.VMEM((2, comps, thirds, times // 2 * BIG, 2 * lanes), F32)],
        compiler_params=pltpu.CompilerParams(vmem_limit_bytes=16 << 20),
        cost_estimate=pl.CostEstimate(
            flops=elements * 4 * lanes, transcendentals=0, bytes_accessed=elements * 6
        ),
        name="inner",
    )(winds, cos_rows)


def outer_kernel(
    step_lon, step_lat, g_ref, pick_ref, near_ref, far_ref, sidea_ref, sideb_ref, cos_ref,
    f_ref, c_ref, prev_s, next_s, halo_s,
):
    levels, _, groups, deep, lanes = g_ref.shape
    times = deep // SUB
    half = times // 2
    thirds = groups // 2
    comps = 2
    units = comps * thirds * 2
    by_lon, by_up, by_down = factors(cos_ref, step_lon, step_lat, (SUB, lanes))
    row = iota((SUB, lanes), 0)
    lane = iota((SUB, lanes), 1)
    by_lat = jnp.where(lane == lanes - 1, by_up, jnp.where(lane == 0, -by_down, 0.0))

    even = parity("lon_2") == 0
    near = near_ref[...].astype(F32)
    far = far_ref[...].astype(F32)
    lon_row = by_lon[0:1, :]
    prev_s[...] = jnp.where(even, far, near) * lon_row
    next_s[...] = jnp.where(even, near, far) * lon_row
    takes = (iota(sidea_ref.shape, 1) + parity("lat")) % 2 == 1
    side = jnp.where(takes, sidea_ref[...].astype(F32), sideb_ref[...].astype(F32))

    def lon_edge(c, t, l, g):
        k = (l * comps + c) * times + t
        if g == 0:
            return jnp.where(row == 0, -prev_s[k : k + 1, :], 0.0)
        if g == groups - 1:
            return jnp.where(row == SUB - 1, next_s[k : k + 1, :], 0.0)
        return None

    def one(t, l):
        h = t // half
        cut = slice(t * SUB, (t + 1) * SUB)
        vort, div = [], []
        for g in range(groups):
            at = (t % half) * BIG + g % 2 * SUB
            lat = []
            for c in range(comps):
                u = unit_of(c, g // 2, h, thirds) * lanes
                lat.append(halo_s[l % 2, at : at + SUB, u : u + lanes] * by_lat)
            first = g_ref[l, 0, g, cut, :] - lat[0]
            second = g_ref[l, 1, g, cut, :] + lat[1]
            if g in (0, groups - 1):
                first = first + lon_edge(1, t, l, g)
                second = second + lon_edge(0, t, l, g)
            vort.append(first)
            div.append(second)
        return vort, div

    total = None
    for l in range(levels):
        mine = side if l == 0 else pltpu.roll(side, lanes - 2 * units * l, 1)
        halo_s[l % 2] = jnp.dot(mine.astype(BF16), pick_ref[...], preferred_element_type=F32)
        for pair in range(times // 2):
            early, late = one(2 * pair, l), one(2 * pair + 1, l)
            at = pair * 2 * SUB
            for s in range(2):
                for g in range(groups):
                    both = jnp.concatenate([early[s][g], late[s][g]], axis=0)
                    f_ref[l, s, g, at : at + 2 * SUB, :] = both.astype(BF16)
        for s in range(2):
            x = jnp.concatenate([f_ref[l, s, g] for g in range(groups)], axis=1)
            term = lax.dot_general(x, x, (((1,), (1,)), ((), ())), preferred_element_type=F32)
            total = term if total is None else total + term

    same = iota((deep, deep), 0) % SUB == iota((deep, deep), 1) % SUB
    kept = jnp.where(same, total, 0.0)
    kept = kept.reshape(times, SUB, deep).sum(axis=1)
    fold = as_bf16(iota((deep, times), 0) // SUB == iota((deep, times), 1))
    cov = jnp.dot(
        jnp.concatenate(three_terms(kept), axis=1),
        jnp.concatenate([fold] * 3, axis=0),
        preferred_element_type=F32,
    )
    c_ref[...] = jnp.concatenate([cov[q * SUB : (q + 1) * SUB] for q in range(times // SUB)], axis=1)


def outer(g, pick, near, far, sidea, sideb, cos_rows, step_lon, step_lat):
    lanes = g.shape[-1]
    whole = pl.BlockSpec(memory_space=pltpu.VMEM)
    return pl.pallas_call(
        functools.partial(outer_kernel, step_lon, step_lat),
        in_specs=[whole] * 7,
        out_specs=[whole, whole],
        out_shape=[pltpu.VMEM(g.shape, BF16), jax.ShapeDtypeStruct((SUB, lanes), F32)],
        scratch_shapes=[
            pltpu.VMEM(near.shape, F32),
            pltpu.VMEM(near.shape, F32),
            pltpu.VMEM((2, sidea.shape[0], pick.shape[1]), F32),
        ],
        compiler_params=pltpu.CompilerParams(vmem_limit_bytes=16 << 20),
        name="outer",
    )(g, pick, near, far, sidea, sideb, cos_rows)


def transform(cov, table, total_rows, lanes):
    times = table.shape[1]
    half = lanes // 2
    table_b = table.astype(BF16)
    left = jnp.dot(
        jnp.concatenate([table_b] * 3, axis=1),
        jnp.concatenate(three_terms(cov), axis=0),
        preferred_element_type=F32,
    )
    gram = lax.dot_general(
        jnp.concatenate(three_terms(left), axis=1),
        jnp.concatenate([table_b] * 3, axis=1),
        (((1,), (1,)), ((), ())),
        preferred_element_type=F32,
    ) / total_rows
    row = iota((COLS, lanes), 0)
    lane = iota((COLS, lanes), 1)
    near = lane < half
    pad = jnp.zeros((COLS, half - COLS - times), F32)
    parts, sizes = [], []
    for f in range(FREQS):
        at = slice(f * COLS, (f + 1) * COLS)
        own = gram[at, at]
        diagonal = iota((COLS, COLS), 0) == iota((COLS, COLS), 1)
        size = jnp.max(jnp.where(diagonal, own, 0.0), axis=(0, 1), keepdims=True)
        sizes.append(size)
        parts += [own / size, table[at], pad]
    a = jnp.concatenate(parts, axis=1)

    for j in range(0, COLS, 2):
        c1 = jnp.where(near, a[:, j : j + 1], a[:, half + j : half + j + 1])
        c2 = jnp.where(near, a[:, j + 1 : j + 2], a[:, half + j + 1 : half + j + 2])
        r1 = a[j : j + 1, :]
        r2 = a[j + 1 : j + 2, :]
        p11 = c1[j : j + 1]
        p12 = c2[j : j + 1]
        p22 = c2[j + 1 : j + 2]
        inverse = 1.0 / (p11 * p22 - p12 * p12)
        s1 = (p22 * r1 - p12 * r2) * inverse
        s2 = (p11 * r2 - p12 * r1) * inverse
        a = jnp.where(row > j + 1, a - c1 * s1 - c2 * s2, a)

    odd = iota((COLS, 1), 0) % 2 == 1
    weights = []
    before = pltpu.roll(a, 1, 0)
    for f in range(FREQS):
        base = f * half
        on = jnp.sum(jnp.where(lane == base + row, a, 0.0), axis=1, keepdims=True)
        off = jnp.sum(jnp.where(lane == base + row - 1, a, 0.0), axis=1, keepdims=True)
        above = jnp.sum(jnp.where(lane == base + row - 1, before, 0.0), axis=1, keepdims=True)
        ratio = jnp.where(odd, off / above, 0.0)
        pivot = on - ratio * off
        cut = slice(base + COLS, base + COLS + times)
        weights.append((a[:, cut] - ratio * before[:, cut]) / jnp.sqrt(pivot) / jnp.sqrt(sizes[f]))
    return jnp.concatenate(weights, axis=0)


def basis_kernel(total_rows, sums_ref, table_ref, f_ref, out_hbm, out_ref, mix_ref, sems):
    levels, kinds, groups, deep, lanes = f_ref.shape
    times = deep // SUB
    outs = FREQS * COLS
    flat = jnp.sum(sums_ref[...], axis=0)
    cov = jnp.concatenate([flat[:, q * times : (q + 1) * times] for q in range(times // SUB)], axis=0)
    w = transform(cov, table_ref[...], total_rows, lanes)
    w_hi = w.astype(BF16)
    w_lo = (w - w_hi.astype(F32)).astype(BF16)
    spread = as_bf16(iota((outs * SUB, outs), 0) // SUB == iota((outs * SUB, outs), 1))
    widen = as_bf16(iota((times, deep), 0) == iota((times, deep), 1) // SUB)
    same = iota((outs * SUB, deep), 0) % SUB == iota((outs * SUB, deep), 1) % SUB
    for k, term in enumerate((w_hi, w_lo)):
        tall = jnp.dot(spread, term, preferred_element_type=F32).astype(BF16)
        full = jnp.dot(tall, widen, preferred_element_type=F32)
        mix_ref[:, k * deep : (k + 1) * deep] = jnp.where(same, full, 0.0).astype(BF16)

    @pl.loop(0, levels)
    def _(l):
        for s in range(kinds):
            for g in range(0, groups, 2):
                x = jnp.concatenate([f_ref[l, s, g], f_ref[l, s, g + 1]], axis=1)
                x = jnp.concatenate([x, x], axis=0)
                y = jnp.dot(mix_ref[...], x, preferred_element_type=F32)
                for e in range(2):
                    part = y[:, e * lanes : (e + 1) * lanes].reshape(outs, SUB, lanes)
                    out_ref[:, s, l, (g + e) * SUB : (g + e + 1) * SUB, :] = part
            pltpu.make_async_copy(out_ref.at[:, s, l], out_hbm.at[:, s, l], sems.at[s, l]).start()

    for l in range(levels):
        for s in range(kinds):
            pltpu.make_async_copy(out_ref.at[:, s, l], out_hbm.at[:, s, l], sems.at[s, l]).wait()


def basis_of(sums, table, f, total_rows):
    levels, kinds, groups, deep, lanes = f.shape
    outs = FREQS * COLS
    whole = pl.BlockSpec(memory_space=pltpu.VMEM)
    out_shape = (outs, kinds, levels, groups * SUB, lanes)
    return pl.pallas_call(
        functools.partial(basis_kernel, total_rows),
        in_specs=[whole, whole, whole],
        out_specs=pl.BlockSpec(memory_space=pltpu.HBM),
        out_shape=pltpu.HBM(out_shape, F32),
        scratch_shapes=[
            pltpu.VMEM(out_shape, F32),
            pltpu.VMEM((outs * SUB, 2 * deep), BF16),
            pltpu.SemaphoreType.DMA((kinds, levels)),
        ],
        compiler_params=pltpu.CompilerParams(vmem_limit_bytes=16 << 20),
        name="basis",
    )(sums, table, f)


def exchange(x, axes):
    copies = jnp.broadcast_to(x, (lax.axis_size(axes), *x.shape))
    return lax.all_to_all(copies, axes, split_axis=0, concat_axis=0, tiled=True)


def swap(x, axes, offset):
    size = lax.axis_size(axes)
    pairs = []
    for i in range(offset, size, 2):
        pairs += [(i, (i + 1) % size), ((i + 1) % size, i)]
    return lax.ppermute(x, axes, pairs)


def body(winds):
    _, times, levels, lon_cells, lat_cells = winds.shape
    grid_lon = lon_cells * lax.axis_size(LON)
    grid_lat = lat_cells * lax.axis_size("lat")
    step_lon = 2.0 * math.pi / grid_lon
    step_lat = 2.6 / grid_lat
    near, far, cols, winds = pack(winds)
    near = swap(near, "lon_2", 0)
    far = swap(far, LON, 1)
    sidea = swap(cols, "lat", 0)
    sideb = swap(cols, "lat", 1)
    shape = (SUB, lat_cells)
    index = lax.axis_index("lat") * lat_cells + iota(shape, 1) + iota(shape, 0) - 1
    inside = (index >= 0) & (index < grid_lat)
    cos_rows = jnp.where(inside, jnp.cos(-1.3 + (index.astype(F32) + 0.5) * step_lat), 0.0)
    g, pick = inner(winds, cos_rows, step_lon, step_lat)
    f, cov = outer(g, pick, near, far, sidea, sideb, cos_rows, step_lon, step_lat)
    half_sums = exchange(cov, ("lon_2", "lat")).sum(axis=0)
    sums = exchange(half_sums, ("lon_0", "lon_1"))
    return basis_of(sums, jnp.asarray(taper_table()), f, 2 * levels * grid_lon * grid_lat)


def solution(mesh):
    split = Mesh(
        mesh.devices.reshape(4, 4, 2, mesh.shape["lat"]), ("lon_0", "lon_1", "lon_2", "lat")
    )
    placed = (P(None, None, None, LON, "lat"),)
    return jax.shard_map(
        body,
        mesh=split,
        in_specs=placed,
        out_specs=P(None, None, None, LON, "lat"),
        check_vma=False,
    )
```

time: 59.9 us -> 52 us (0.87)
  waiting for transfers between devices: 3.93 us -> 0.01 us
  local copies, waits for them, and re-layouts: 3.32 us -> 0.02 us
  Pallas kernels: 17.7 us -> 16 us
  blocking collectives: 26.1 us -> 27.2 us
    ppermute x4, waiting for transfers between devices: 3.93 us -> 0.01 us  [swap(): return lax.ppermute(x, axes, pairs)]
    unnamed x8 -> x2, local copies, waits for them, and re-layouts: 3.3 us -> 0.01 us
    all_to_all x2, blocking collectives: 26.1 us -> 27.2 us  [exchange(): return lax.all_to_all(copies, axes, split_axis=0, concat_axis=0, tiled=True)]
    pallas_call x1, Pallas kernels: 7.7 us -> 6.75 us  [basis_of(): pl.pallas_call(functools.partial(basis_kernel, total_rows), in_specs=[who...]
    pallas_call x1 -> x2, Pallas kernels: 6.4 us -> 5.76 us  [the longest x1 3.01 us: inner(): pl.pallas_call(functools.partial(inner_kernel, step_lon, step_lat), in_sp...]
  transfers between devices with their start and end apart: 4 -> 4, of which waited for: 2 -> 0; matrix products, arithmetic and copies ran while one was open for 0% -> 0% of each run, Pallas kernels for 0% -> 6%
where the time goes in v3:
time: 52 us; the launch traced here: 51.9 us
  blocking collectives  27.2 us (52%)
  Pallas kernels  16 us (31%)
  starting transfers between devices  8.56 us (16%)
    all_to_all x2, blocking collectives, exchange(): return lax.all_to_all(copies, axes, split_axis=0, concat_axis=0, tiled=True)  27.2 us
    ppermute x4, starting transfers between devices, swap(): return lax.ppermute(x, axes, pairs)  8.56 us
    pallas_call x1, Pallas kernels, basis_of(): pl.pallas_call(functools.partial(basis_kernel, total_rows), in_specs=[who...  6.75 us
    pallas_call x1, Pallas kernels, pack(): pl.pallas_call(pack_kernel, in_specs=[pl.BlockSpec(memory_space=pltpu.HBM...  3.47 us
    pallas_call x1, Pallas kernels, inner(): pl.pallas_call(functools.partial(inner_kernel, step_lon, step_lat), in_sp...  3.01 us
    pallas_call x1, Pallas kernels, outer(): pl.pallas_call(functools.partial(outer_kernel, step_lon, step_lat), in_sp...  2.75 us
  transfers between devices with their start and end apart: 4, of which 0 were waited for; matrix products, arithmetic and copies ran while one was open for 0% of the time, Pallas kernels for 6%

profile of v3, /device:TPU:1, one launch (start us, length us, event | category | flops | bytes accessed | tf_op | source)
XLA Modules:
  0.0 51.9 jit_solution(5050027565812484070)
XLA Ops:
  0.0 3.5 %pack.1 = (bf16[256,128]{1,0:T(8,128)(2,1)}, bf16[256,128]{1,0:T(8,128)(2,1)S(1)}, bf16[256,128]{1,0:T(8,128)(2,1)S(1)}, bf16[2,32,4,48,128]{4,3,2,1,0:T(8,128)(2,1)S(1)}) custom-call(bf16[2,32,4,48,128]{4,3,2,1,0:T(8,128)(2,1)} %w_hbm.1), custom_call_target="tpu_custom_call" | custom-call | tf_op jit(solution)/shard_map/pack/pallas_call | solution.py:112
  3.5 6.5 %collective-permute-start.3 = (bf16[256,128]{1,0:T(8,128)(2,1)S(1)}, bf16[256,128]{1,0:T(8,128)(2,1)S(1)}, u32[]{:S(2)}, u32[]{:S(2)}) collective-permute-start(bf16[256,128]{1,0:T(8,128)(2,1)S(1)} %get-tuple-element.18), channel_id=1, source_target_pairs={{1,2},{2,1},{3,4},{4,3},{5,6},{6,5},{7,0},{0,7},{9,10},{10,9},{11,... | collective-permute-start | bytes 196616 | tf_op jit(solution)/shard_map/ppermute | solution.py:427
  10.0 0.0 collective-permute-start.2
  10.0 1.0 %collective-permute-start = (bf16[256,128]{1,0:T(8,128)(2,1)}, bf16[256,128]{1,0:T(8,128)(2,1)S(1)}, u32[]{:S(2)}, u32[]{:S(2)}) collective-permute-start(bf16[256,128]{1,0:T(8,128)(2,1)} %get-tuple-element.16), channel_id=1, source_target_pairs={{0,8},{8,0},{1,9},{9,1},{2,10},{10,2},{3,11},{11,3},{4,12},{12,4},... | collective-permute-start | bytes 196616 | tf_op jit(solution)/shard_map/ppermute | solution.py:427
  10.9 1.1 %collective-permute-start.1 = (bf16[256,128]{1,0:T(8,128)(2,1)S(1)}, bf16[256,128]{1,0:T(8,128)(2,1)S(1)}, u32[]{:S(2)}, u32[]{:S(2)}) collective-permute-start(bf16[256,128]{1,0:T(8,128)(2,1)S(1)} %get-tuple-element.17), channel_id=1, source_target_pairs={{8,16},{16,8},{24,32},{32,24},{40,48},{48,40},{56,64},{64,56},{72,... | collective-permute-start | bytes 196616 | tf_op jit(solution)/shard_map/ppermute | solution.py:427
  12.0 0.1 cosine_select_fusion.cos_ref
  12.1 3.0 %inner.1 = (f32[4,2,6,256,128]{4,3,2,1,0:T(8,128)S(1)}, bf16[128,1536]{1,0:T(8,128)(2,1)S(1)}) custom-call(bf16[2,32,4,48,128]{4,3,2,1,0:T(8,128)(2,1)S(1)} %get-tuple-element.13.w_ref, f32[8,128]{1,0:T(8,128)S(1)} %cosine_select_fusion.cos_ref), custom_call_target="tpu_custom_call" | custom-call | flops 805306368 | bytes 9437184 | tf_op jit(solution)/shard_map/inner/pallas_call | solution.py:192
  15.1 0.0 collective-permute-done.near_ref
  15.1 0.0 collective-permute-done.1.far_ref
  15.1 0.0 collective-permute-done.3.sideb_ref
  15.1 0.0 collective-permute-done.2.sidea_ref
  15.2 0.0 copy-start
  15.2 2.7 %outer.1 = (bf16[4,2,6,256,128]{4,3,2,1,0:T(8,128)(2,1)S(1)}, f32[8,128]{1,0:T(8,128)S(1)}) custom-call(f32[4,2,6,256,128]{4,3,2,1,0:T(8,128)S(1)} %get-tuple-element.14.g_ref, bf16[128,1536]{1,0:T(8,128)(2,1)S(1)} %get-tuple-element.15.pick_ref, bf16[256,128]{1,0:T(8,128)(2,1)S(1)} %collective-permute-done.near_ref, ...), custom_call_target="tpu_custom_call" | custom-call | tf_op jit(solution)/shard_map/outer/pallas_call | solution.py:291
  17.9 15.8 %all_to_all.10 = f32[16,8,128]{2,1,0:T(8,128)S(1)} all-to-all(f32[16,8,128]{2,1,0:T(8,128)S(1)} %broadcast_in_dim.11), channel_id=1, replica_groups=mesh['lon_0'=4,'lon_1'=4,'lon_2'=2,'lat'=8] {'lon_2','lat'}, dimensions={0} | all-to-all | bytes 131072 | tf_op jit(solution)/shard_map/all_to_all | solution.py:419
  33.8 11.3 %all_to_all.11.sums_ref = f32[16,8,128]{2,1,0:T(8,128)S(1)} all-to-all(f32[16,8,128]{2,1,0:T(8,128)S(1)} %broadcast_in_dim.12), channel_id=1, replica_groups=mesh['lon_0'=4,'lon_1'=4,'lon_2'=2,'lat'=8] {'lon_0','lon_1'}, dimensions={0} | all-to-all | bytes 131072 | tf_op jit(solution)/shard_map/all_to_all | solution.py:419
  45.1 0.0 copy-done
  45.1 6.8 %basis.1 = f32[48,2,4,48,128]{4,3,2,1,0:T(8,128)} custom-call(f32[16,8,128]{2,1,0:T(8,128)S(1)} %all_to_all.11.sums_ref, f32[48,32]{1,0:T(8,128)S(1)} %copy-done, bf16[4,2,6,256,128]{4,3,2,1,0:T(8,128)(2,1)S(1)} %get-tuple-element.20.f_ref), custom_call_target="tpu_custom_call" | custom-call | tf_op jit(solution)/shard_map/basis/pallas_call | solution.py:402
  (4 shorter events, 0.0 us)
Async XLA Ops:
  3.5 11.7 %collective-permute-start.3 = (bf16[256,128]{1,0:T(8,128)(2,1)S(1)}, bf16[256,128]{1,0:T(8,128)(2,1)S(1)}, u32[]{:S(2)}, u32[]{:S(2)}) collective-permute-start(bf16[256,128]{1,0:T(8,128)(2,1)S(1)} %get-tuple-element.18), channel_id=1, source_target_pairs={{1,2},{2,1},{3,4},{4,3},{5,6},{6,5},{7,0},{0,7},{9,10},{10,9},{11,... | collective-permute-start | bytes 196616 | tf_op jit(solution)/shard_map/ppermute | solution.py:427
  10.0 5.2 %collective-permute-start.2 = (bf16[256,128]{1,0:T(8,128)(2,1)S(1)}, bf16[256,128]{1,0:T(8,128)(2,1)S(1)}, u32[]{:S(2)}, u32[]{:S(2)}) collective-permute-start(bf16[256,128]{1,0:T(8,128)(2,1)S(1)} %get-tuple-element.18), channel_id=1, source_target_pairs={{0,1},{1,0},{2,3},{3,2},{4,5},{5,4},{6,7},{7,6},{8,9},{9,8},{10,11... | collective-permute-start | bytes 196616 | tf_op jit(solution)/shard_map/ppermute | solution.py:427
  10.0 5.1 %collective-permute-start = (bf16[256,128]{1,0:T(8,128)(2,1)}, bf16[256,128]{1,0:T(8,128)(2,1)S(1)}, u32[]{:S(2)}, u32[]{:S(2)}) collective-permute-start(bf16[256,128]{1,0:T(8,128)(2,1)} %get-tuple-element.16), channel_id=1, source_target_pairs={{0,8},{8,0},{1,9},{9,1},{2,10},{10,2},{3,11},{11,3},{4,12},{12,4},... | collective-permute-start | bytes 196616 | tf_op jit(solution)/shard_map/ppermute | solution.py:427
  10.9 4.2 %collective-permute-start.1 = (bf16[256,128]{1,0:T(8,128)(2,1)S(1)}, bf16[256,128]{1,0:T(8,128)(2,1)S(1)}, u32[]{:S(2)}, u32[]{:S(2)}) collective-permute-start(bf16[256,128]{1,0:T(8,128)(2,1)S(1)} %get-tuple-element.17), channel_id=1, source_target_pairs={{8,16},{16,8},{24,32},{32,24},{40,48},{48,40},{56,64},{64,56},{72,... | collective-permute-start | bytes 196616 | tf_op jit(solution)/shard_map/ppermute | solution.py:427
  15.2 30.0 %copy-start = (f32[48,32]{1,0:T(8,128)S(1)}, f32[48,32]{1,0:T(8,128)}, u32[]{:S(2)}) copy-start(f32[48,32]{1,0:T(8,128)} %constant.23.clone.table_ref) | copy-start | bytes 18436

commit v4 on v3

--- a/solution.py
+++ b/solution.py
@@ -70,30 +70,39 @@
     half = times // 2
     thirds = rows // BIG
     units = comps * thirds * 2
-    copies = [
-        pltpu.make_async_copy(w_hbm.at[:, :, l], w_ref.at[:, :, l], sems.at[l]) for l in range(levels)
-    ]
-    for copy in copies:
-        copy.start()
+    copies = {}
+    for l in range(levels):
+        for h in range(2):
+            cut = pl.ds(h * half, half)
+            copies[l, h] = pltpu.make_async_copy(
+                w_hbm.at[:, cut, l], w_ref.at[:, cut, l], sems.at[l, h]
+            )
+            copies[l, h].start()
     deep = half * BIG
-    at = iota((units * lanes, lanes), 0)
-    spot = iota((units * lanes, lanes), 1)
+    chunk = comps * thirds
+    at = iota((chunk * lanes, lanes), 0)
+    spot = iota((chunk * lanes, lanes), 1)
     here = at % lanes
-    want = at // lanes * 2
-    hit = as_bf16(((here == lanes - 1) & (spot == want)) | ((here == 0) & (spot == want + 1)))
+    want = at // lanes * 4
+    hits = []
+    for h in range(2):
+        lower = want + 2 * h
+        hits.append(as_bf16(((here == lanes - 1) & (spot == lower)) | ((here == 0) & (spot == lower + 1))))
     for l in range(levels):
-        copies[l].wait()
-        pieces = []
-        for c in range(comps):
-            for g in range(thirds):
-                for h in range(2):
+        total = None
+        for h in range(2):
+            copies[l, h].wait()
+            pieces = []
+            for c in range(comps):
+                for g in range(thirds):
                     x = w_ref[c, h * half : (h + 1) * half, l, g * BIG : (g + 1) * BIG, :]
                     pieces.append(x.reshape(deep, lanes))
-            for t in range(times):
-                k = (l * comps + c) * times + t
-                first_s[k : k + 1, :] = w_ref[c, t, l, 0:BIG, :].astype(F32)[0:1]
-                last_s[k : k + 1, :] = w_ref[c, t, l, rows - BIG : rows, :].astype(F32)[BIG - 1 : BIG]
-        total = jnp.dot(jnp.concatenate(pieces, axis=1), hit, preferred_element_type=F32)
+                for t in range(h * half, (h + 1) * half):
+                    k = (l * comps + c) * times + t
+                    first_s[k : k + 1, :] = w_ref[c, t, l, 0:BIG, :].astype(F32)[0:1]
+                    last_s[k : k + 1, :] = w_ref[c, t, l, rows - BIG : rows, :].astype(F32)[BIG - 1 : BIG]
+            term = jnp.dot(jnp.concatenate(pieces, axis=1), hits[h], preferred_element_type=F32)
+            total = term if total is None else total + term
         if l == 0:
             acc_ref[...] = total
         else:
@@ -119,7 +128,7 @@
             pltpu.VMEM((many, lanes), F32),
             pltpu.VMEM((many, lanes), F32),
             pltpu.VMEM((deep, lanes), F32),
-            pltpu.SemaphoreType.DMA((levels,)),
+            pltpu.SemaphoreType.DMA((levels, 2)),
         ],
         compiler_params=pltpu.CompilerParams(vmem_limit_bytes=16 << 20),
         name="pack",
@@ -419,10 +428,10 @@
     return lax.all_to_all(copies, axes, split_axis=0, concat_axis=0, tiled=True)
 
 
-def swap(x, axes, offset):
+def swap(x, axes, offset, around=True):
     size = lax.axis_size(axes)
     pairs = []
-    for i in range(offset, size, 2):
+    for i in range(offset, size if around else size - 1, 2):
         pairs += [(i, (i + 1) % size), ((i + 1) % size, i)]
     return lax.ppermute(x, axes, pairs)
 
@@ -437,7 +446,7 @@
     near = swap(near, "lon_2", 0)
     far = swap(far, LON, 1)
     sidea = swap(cols, "lat", 0)
-    sideb = swap(cols, "lat", 1)
+    sideb = swap(cols, "lat", 1, around=False)
     shape = (SUB, lat_cells)
     index = lax.axis_index("lat") * lat_cells + iota(shape, 1) + iota(shape, 0) - 1
     inside = (index >= 0) & (index < grid_lat)

time: 52 us -> 54.1 us (1.040)
  blocking collectives: 27.2 us -> 29.2 us
    all_to_all x2, blocking collectives: 27.2 us -> 29.2 us  [exchange(): return lax.all_to_all(copies, axes, split_axis=0, concat_axis=0, tiled=True)]
where the time goes in v4:
time: 54.1 us; the launch traced here: 53.9 us
  blocking collectives  29.2 us (54%)
  Pallas kernels  16.1 us (30%)
  starting transfers between devices  8.45 us (16%)
    all_to_all x2, blocking collectives, exchange(): return lax.all_to_all(copies, axes, split_axis=0, concat_axis=0, tiled=True)  29.2 us
    ppermute x4, starting transfers between devices, swap(): return lax.ppermute(x, axes, pairs)  8.45 us
    pallas_call x1, Pallas kernels, basis_of(): pl.pallas_call(functools.partial(basis_kernel, total_rows), in_specs=[who...  6.75 us
    pallas_call x1, Pallas kernels, pack(): pl.pallas_call(pack_kernel, in_specs=[pl.BlockSpec(memory_space=pltpu.HBM...  3.6 us
    pallas_call x1, Pallas kernels, inner(): pl.pallas_call(functools.partial(inner_kernel, step_lon, step_lat), in_sp...  2.99 us
    pallas_call x1, Pallas kernels, outer(): pl.pallas_call(functools.partial(outer_kernel, step_lon, step_lat), in_sp...  2.75 us
  transfers between devices with their start and end apart: 4, of which 0 were waited for; matrix products, arithmetic and copies ran while one was open for 0% of the time, Pallas kernels for 6%

profile of v4, /device:TPU:1, one launch (start us, length us, event | category | flops | bytes accessed | tf_op | source)
XLA Modules:
  0.0 53.9 jit_solution(8598047472483575262)
XLA Ops:
  0.0 3.6 %pack.1 = (bf16[256,128]{1,0:T(8,128)(2,1)}, bf16[256,128]{1,0:T(8,128)(2,1)S(1)}, bf16[256,128]{1,0:T(8,128)(2,1)S(1)}, bf16[2,32,4,48,128]{4,3,2,1,0:T(8,128)(2,1)S(1)}) custom-call(bf16[2,32,4,48,128]{4,3,2,1,0:T(8,128)(2,1)} %w_hbm.1), custom_call_target="tpu_custom_call" | custom-call | tf_op jit(solution)/shard_map/pack/pallas_call | solution.py:121
  3.6 0.7 %collective-permute-start.3 = (bf16[256,128]{1,0:T(8,128)(2,1)S(1)}, bf16[256,128]{1,0:T(8,128)(2,1)S(1)}, u32[]{:S(2)}, u32[]{:S(2)}) collective-permute-start(bf16[256,128]{1,0:T(8,128)(2,1)S(1)} %get-tuple-element.18), channel_id=1, source_target_pairs={{1,2},{2,1},{3,4},{4,3},{5,6},{6,5},{9,10},{10,9},{11,12},{12,11},... | collective-permute-start | bytes 196616 | tf_op jit(solution)/shard_map/ppermute | solution.py:436
  4.3 5.4 %collective-permute-start.2 = (bf16[256,128]{1,0:T(8,128)(2,1)S(1)}, bf16[256,128]{1,0:T(8,128)(2,1)S(1)}, u32[]{:S(2)}, u32[]{:S(2)}) collective-permute-start(bf16[256,128]{1,0:T(8,128)(2,1)S(1)} %get-tuple-element.18), channel_id=1, source_target_pairs={{0,1},{1,0},{2,3},{3,2},{4,5},{5,4},{6,7},{7,6},{8,9},{9,8},{10,11... | collective-permute-start | bytes 196616 | tf_op jit(solution)/shard_map/ppermute | solution.py:436
  9.7 1.2 %collective-permute-start = (bf16[256,128]{1,0:T(8,128)(2,1)}, bf16[256,128]{1,0:T(8,128)(2,1)S(1)}, u32[]{:S(2)}, u32[]{:S(2)}) collective-permute-start(bf16[256,128]{1,0:T(8,128)(2,1)} %get-tuple-element.16), channel_id=1, source_target_pairs={{0,8},{8,0},{1,9},{9,1},{2,10},{10,2},{3,11},{11,3},{4,12},{12,4},... | collective-permute-start | bytes 196616 | tf_op jit(solution)/shard_map/ppermute | solution.py:436
  11.0 1.1 %collective-permute-start.1 = (bf16[256,128]{1,0:T(8,128)(2,1)S(1)}, bf16[256,128]{1,0:T(8,128)(2,1)S(1)}, u32[]{:S(2)}, u32[]{:S(2)}) collective-permute-start(bf16[256,128]{1,0:T(8,128)(2,1)S(1)} %get-tuple-element.17), channel_id=1, source_target_pairs={{8,16},{16,8},{24,32},{32,24},{40,48},{48,40},{56,64},{64,56},{72,... | collective-permute-start | bytes 196616 | tf_op jit(solution)/shard_map/ppermute | solution.py:436
  12.1 0.1 cosine_select_fusion.cos_ref
  12.1 3.0 %inner.1 = (f32[4,2,6,256,128]{4,3,2,1,0:T(8,128)S(1)}, bf16[128,1536]{1,0:T(8,128)(2,1)S(1)}) custom-call(bf16[2,32,4,48,128]{4,3,2,1,0:T(8,128)(2,1)S(1)} %get-tuple-element.13.w_ref, f32[8,128]{1,0:T(8,128)S(1)} %cosine_select_fusion.cos_ref), custom_call_target="tpu_custom_call" | custom-call | flops 805306368 | bytes 9437184 | tf_op jit(solution)/shard_map/inner/pallas_call | solution.py:201
  15.1 0.0 collective-permute-done.near_ref
  15.1 0.0 collective-permute-done.1.far_ref
  15.1 0.0 collective-permute-done.3.sideb_ref
  15.1 0.0 collective-permute-done.2.sidea_ref
  15.2 0.0 copy-start
  15.2 2.7 %outer.1 = (bf16[4,2,6,256,128]{4,3,2,1,0:T(8,128)(2,1)S(1)}, f32[8,128]{1,0:T(8,128)S(1)}) custom-call(f32[4,2,6,256,128]{4,3,2,1,0:T(8,128)S(1)} %get-tuple-element.14.g_ref, bf16[128,1536]{1,0:T(8,128)(2,1)S(1)} %get-tuple-element.15.pick_ref, bf16[256,128]{1,0:T(8,128)(2,1)S(1)} %collective-permute-done.near_ref, ...), custom_call_target="tpu_custom_call" | custom-call | tf_op jit(solution)/shard_map/outer/pallas_call | solution.py:300
  17.9 17.8 %all_to_all.10 = f32[16,8,128]{2,1,0:T(8,128)S(1)} all-to-all(f32[16,8,128]{2,1,0:T(8,128)S(1)} %broadcast_in_dim.11), channel_id=1, replica_groups=mesh['lon_0'=4,'lon_1'=4,'lon_2'=2,'lat'=8] {'lon_2','lat'}, dimensions={0} | all-to-all | bytes 131072 | tf_op jit(solution)/shard_map/all_to_all | solution.py:428
  35.8 11.4 %all_to_all.11.sums_ref = f32[16,8,128]{2,1,0:T(8,128)S(1)} all-to-all(f32[16,8,128]{2,1,0:T(8,128)S(1)} %broadcast_in_dim.12), channel_id=1, replica_groups=mesh['lon_0'=4,'lon_1'=4,'lon_2'=2,'lat'=8] {'lon_0','lon_1'}, dimensions={0} | all-to-all | bytes 131072 | tf_op jit(solution)/shard_map/all_to_all | solution.py:428
  47.2 0.0 copy-done
  47.2 6.8 %basis.1 = f32[48,2,4,48,128]{4,3,2,1,0:T(8,128)} custom-call(f32[16,8,128]{2,1,0:T(8,128)S(1)} %all_to_all.11.sums_ref, f32[48,32]{1,0:T(8,128)S(1)} %copy-done, bf16[4,2,6,256,128]{4,3,2,1,0:T(8,128)(2,1)S(1)} %get-tuple-element.20.f_ref), custom_call_target="tpu_custom_call" | custom-call | tf_op jit(solution)/shard_map/basis/pallas_call | solution.py:411
  (4 shorter events, 0.0 us)
Async XLA Ops:
  3.6 11.5 %collective-permute-start.3 = (bf16[256,128]{1,0:T(8,128)(2,1)S(1)}, bf16[256,128]{1,0:T(8,128)(2,1)S(1)}, u32[]{:S(2)}, u32[]{:S(2)}) collective-permute-start(bf16[256,128]{1,0:T(8,128)(2,1)S(1)} %get-tuple-element.18), channel_id=1, source_target_pairs={{1,2},{2,1},{3,4},{4,3},{5,6},{6,5},{9,10},{10,9},{11,12},{12,11},... | collective-permute-start | bytes 196616 | tf_op jit(solution)/shard_map/ppermute | solution.py:436
  4.3 10.9 %collective-permute-start.2 = (bf16[256,128]{1,0:T(8,128)(2,1)S(1)}, bf16[256,128]{1,0:T(8,128)(2,1)S(1)}, u32[]{:S(2)}, u32[]{:S(2)}) collective-permute-start(bf16[256,128]{1,0:T(8,128)(2,1)S(1)} %get-tuple-element.18), channel_id=1, source_target_pairs={{0,1},{1,0},{2,3},{3,2},{4,5},{5,4},{6,7},{7,6},{8,9},{9,8},{10,11... | collective-permute-start | bytes 196616 | tf_op jit(solution)/shard_map/ppermute | solution.py:436
  9.7 5.4 %collective-permute-start = (bf16[256,128]{1,0:T(8,128)(2,1)}, bf16[256,128]{1,0:T(8,128)(2,1)S(1)}, u32[]{:S(2)}, u32[]{:S(2)}) collective-permute-start(bf16[256,128]{1,0:T(8,128)(2,1)} %get-tuple-element.16), channel_id=1, source_target_pairs={{0,8},{8,0},{1,9},{9,1},{2,10},{10,2},{3,11},{11,3},{4,12},{12,4},... | collective-permute-start | bytes 196616 | tf_op jit(solution)/shard_map/ppermute | solution.py:436
  11.0 4.2 %collective-permute-start.1 = (bf16[256,128]{1,0:T(8,128)(2,1)S(1)}, bf16[256,128]{1,0:T(8,128)(2,1)S(1)}, u32[]{:S(2)}, u32[]{:S(2)}) collective-permute-start(bf16[256,128]{1,0:T(8,128)(2,1)S(1)} %get-tuple-element.17), channel_id=1, source_target_pairs={{8,16},{16,8},{24,32},{32,24},{40,48},{48,40},{56,64},{64,56},{72,... | collective-permute-start | bytes 196616 | tf_op jit(solution)/shard_map/ppermute | solution.py:436
  15.2 32.0 %copy-start = (f32[48,32]{1,0:T(8,128)S(1)}, f32[48,32]{1,0:T(8,128)}, u32[]{:S(2)}) copy-start(f32[48,32]{1,0:T(8,128)} %constant.23.clone.table_ref) | copy-start | bytes 18436

commit v5 on v3

--- a/solution.py
+++ b/solution.py
@@ -436,6 +436,7 @@
     near, far, cols, winds = pack(winds)
     near = swap(near, "lon_2", 0)
     far = swap(far, LON, 1)
+    cols, near = lax.optimization_barrier((cols, near))
     sidea = swap(cols, "lat", 0)
     sideb = swap(cols, "lat", 1)
     shape = (SUB, lat_cells)

time: 52 us -> 49.7 us (0.956)
  blocking collectives: 27.2 us -> 25.4 us
  starting transfers between devices: 8.56 us -> 7.62 us
  waiting for transfers between devices: 0.01 us -> 0.93 us
  Pallas kernels: 16 us -> 15.4 us
    all_to_all x2, blocking collectives: 27.2 us -> 25.4 us  [exchange(): return lax.all_to_all(copies, axes, split_axis=0, concat_axis=0, tiled=True)]
    ppermute x4, starting transfers between devices: 8.56 us -> 7.62 us  [swap(): return lax.ppermute(x, axes, pairs)]
    ppermute x4, waiting for transfers between devices: 0.01 us -> 0.93 us  [swap(): return lax.ppermute(x, axes, pairs)]
    pallas_call x1, Pallas kernels: 3.47 us -> 2.9 us  [pack(): pl.pallas_call(pack_kernel, in_specs=[pl.BlockSpec(memory_space=pltpu.HBM...]
  transfers between devices with their start and end apart: 4 -> 4, of which waited for: 0 -> 2; matrix products, arithmetic and copies ran while one was open for 0% -> 0% of each run, Pallas kernels for 6% -> 6%
where the time goes in v5:
time: 49.7 us; the launch traced here: 49.5 us
  blocking collectives  25.4 us (51%)
  Pallas kernels  15.4 us (31%)
  starting transfers between devices  7.62 us (15%)
  waiting for transfers between devices  0.93 us (2%)
    all_to_all x2, blocking collectives, exchange(): return lax.all_to_all(copies, axes, split_axis=0, concat_axis=0, tiled=True)  25.4 us
    ppermute x4, starting transfers between devices, swap(): return lax.ppermute(x, axes, pairs)  7.62 us
    pallas_call x1, Pallas kernels, basis_of(): pl.pallas_call(functools.partial(basis_kernel, total_rows), in_specs=[who...  6.77 us
    pallas_call x1, Pallas kernels, inner(): pl.pallas_call(functools.partial(inner_kernel, step_lon, step_lat), in_sp...  3 us
    pallas_call x1, Pallas kernels, pack(): pl.pallas_call(pack_kernel, in_specs=[pl.BlockSpec(memory_space=pltpu.HBM...  2.9 us
    pallas_call x1, Pallas kernels, outer(): pl.pallas_call(functools.partial(outer_kernel, step_lon, step_lat), in_sp...  2.74 us
  transfers between devices with their start and end apart: 4, of which 2 were waited for; matrix products, arithmetic and copies ran while one was open for 0% of the time, Pallas kernels for 6%

profile of v5, /device:TPU:1, one launch (start us, length us, event | category | flops | bytes accessed | tf_op | source)
XLA Modules:
  0.0 49.5 jit_solution(9329289297839679376)
XLA Ops:
  0.0 2.9 %pack.1 = (bf16[256,128]{1,0:T(8,128)(2,1)S(1)}, bf16[256,128]{1,0:T(8,128)(2,1)S(1)}, bf16[256,128]{1,0:T(8,128)(2,1)S(1)}, bf16[2,32,4,48,128]{4,3,2,1,0:T(8,128)(2,1)S(1)}) custom-call(bf16[2,32,4,48,128]{4,3,2,1,0:T(8,128)(2,1)} %w_hbm.1), custom_call_target="tpu_custom_call" | custom-call | tf_op jit(solution)/shard_map/pack/pallas_call | solution.py:112
  2.9 3.3 %collective-permute-start = (bf16[256,128]{1,0:T(8,128)(2,1)S(1)}, bf16[256,128]{1,0:T(8,128)(2,1)S(1)}, u32[]{:S(2)}, u32[]{:S(2)}) collective-permute-start(bf16[256,128]{1,0:T(8,128)(2,1)S(1)} %get-tuple-element.19), channel_id=1, source_target_pairs={{0,8},{8,0},{1,9},{9,1},{2,10},{10,2},{3,11},{11,3},{4,12},{12,4},... | collective-permute-start | bytes 196616 | tf_op jit(solution)/shard_map/ppermute | solution.py:427
  6.2 0.0 collective-permute-start.1
  6.2 0.1 cosine_select_fusion.cos_ref
  6.3 0.8 %collective-permute-done.near_ref = bf16[256,128]{1,0:T(8,128)(2,1)S(1)} collective-permute-done((bf16[256,128]{1,0:T(8,128)(2,1)S(1)}, bf16[256,128]{1,0:T(8,128)(2,1)S(1)}, u32[]{:S(2)}, u32[]{:S(2)}) %collective-permute-start) | collective-permute-done | bytes 65568 | tf_op jit(solution)/shard_map/ppermute | solution.py:427
  7.1 4.3 %collective-permute-start.3 = (bf16[256,128]{1,0:T(8,128)(2,1)S(1)}, bf16[256,128]{1,0:T(8,128)(2,1)S(1)}, u32[]{:S(2)}, u32[]{:S(2)}) collective-permute-start(bf16[256,128]{1,0:T(8,128)(2,1)S(1)} %get-tuple-element.22), channel_id=1, source_target_pairs={{1,2},{2,1},{3,4},{4,3},{5,6},{6,5},{7,0},{0,7},{9,10},{10,9},{11,... | collective-permute-start | bytes 196616 | tf_op jit(solution)/shard_map/ppermute | solution.py:427
  11.4 0.0 collective-permute-start.2
  11.4 3.0 %inner.1 = (f32[4,2,6,256,128]{4,3,2,1,0:T(8,128)S(1)}, bf16[128,1536]{1,0:T(8,128)(2,1)S(1)}) custom-call(bf16[2,32,4,48,128]{4,3,2,1,0:T(8,128)(2,1)S(1)} %get-tuple-element.15.w_ref, f32[8,128]{1,0:T(8,128)S(1)} %cosine_select_fusion.cos_ref), custom_call_target="tpu_custom_call" | custom-call | flops 805306368 | bytes 9437184 | tf_op jit(solution)/shard_map/inner/pallas_call | solution.py:192
  14.4 0.0 collective-permute-done.1.far_ref
  14.5 0.0 collective-permute-done.3.sideb_ref
  14.5 0.1 collective-permute-done.2.sidea_ref
  14.5 0.0 copy-start
  14.5 2.7 %outer.1 = (bf16[4,2,6,256,128]{4,3,2,1,0:T(8,128)(2,1)S(1)}, f32[8,128]{1,0:T(8,128)S(1)}) custom-call(f32[4,2,6,256,128]{4,3,2,1,0:T(8,128)S(1)} %get-tuple-element.16.g_ref, bf16[128,1536]{1,0:T(8,128)(2,1)S(1)} %get-tuple-element.17.pick_ref, bf16[256,128]{1,0:T(8,128)(2,1)S(1)} %collective-permute-done.near_ref, ...), custom_call_target="tpu_custom_call" | custom-call | tf_op jit(solution)/shard_map/outer/pallas_call | solution.py:291
  17.3 16.4 %all_to_all.10 = f32[16,8,128]{2,1,0:T(8,128)S(1)} all-to-all(f32[16,8,128]{2,1,0:T(8,128)S(1)} %broadcast_in_dim.11), channel_id=1, replica_groups=mesh['lon_0'=4,'lon_1'=4,'lon_2'=2,'lat'=8] {'lon_2','lat'}, dimensions={0} | all-to-all | bytes 131072 | tf_op jit(solution)/shard_map/all_to_all | solution.py:419
  33.7 9.1 %all_to_all.11.sums_ref = f32[16,8,128]{2,1,0:T(8,128)S(1)} all-to-all(f32[16,8,128]{2,1,0:T(8,128)S(1)} %broadcast_in_dim.12), channel_id=1, replica_groups=mesh['lon_0'=4,'lon_1'=4,'lon_2'=2,'lat'=8] {'lon_0','lon_1'}, dimensions={0} | all-to-all | bytes 131072 | tf_op jit(solution)/shard_map/all_to_all | solution.py:419
  42.8 0.0 copy-done
  42.8 6.8 %basis.1 = f32[48,2,4,48,128]{4,3,2,1,0:T(8,128)} custom-call(f32[16,8,128]{2,1,0:T(8,128)S(1)} %all_to_all.11.sums_ref, f32[48,32]{1,0:T(8,128)S(1)} %copy-done, bf16[4,2,6,256,128]{4,3,2,1,0:T(8,128)(2,1)S(1)} %get-tuple-element.24.f_ref), custom_call_target="tpu_custom_call" | custom-call | tf_op jit(solution)/shard_map/basis/pallas_call | solution.py:402
  (4 shorter events, 0.0 us)
Async XLA Ops:
  2.9 4.2 %collective-permute-start = (bf16[256,128]{1,0:T(8,128)(2,1)S(1)}, bf16[256,128]{1,0:T(8,128)(2,1)S(1)}, u32[]{:S(2)}, u32[]{:S(2)}) collective-permute-start(bf16[256,128]{1,0:T(8,128)(2,1)S(1)} %get-tuple-element.19), channel_id=1, source_target_pairs={{0,8},{8,0},{1,9},{9,1},{2,10},{10,2},{3,11},{11,3},{4,12},{12,4},... | collective-permute-start | bytes 196616 | tf_op jit(solution)/shard_map/ppermute | solution.py:427
  6.2 8.2 %collective-permute-start.1 = (bf16[256,128]{1,0:T(8,128)(2,1)S(1)}, bf16[256,128]{1,0:T(8,128)(2,1)S(1)}, u32[]{:S(2)}, u32[]{:S(2)}) collective-permute-start(bf16[256,128]{1,0:T(8,128)(2,1)S(1)} %get-tuple-element.21), channel_id=1, source_target_pairs={{8,16},{16,8},{24,32},{32,24},{40,48},{48,40},{56,64},{64,56},{72,... | collective-permute-start | bytes 196616 | tf_op jit(solution)/shard_map/ppermute | solution.py:427
  7.1 7.3 %collective-permute-start.3 = (bf16[256,128]{1,0:T(8,128)(2,1)S(1)}, bf16[256,128]{1,0:T(8,128)(2,1)S(1)}, u32[]{:S(2)}, u32[]{:S(2)}) collective-permute-start(bf16[256,128]{1,0:T(8,128)(2,1)S(1)} %get-tuple-element.22), channel_id=1, source_target_pairs={{1,2},{2,1},{3,4},{4,3},{5,6},{6,5},{7,0},{0,7},{9,10},{10,9},{11,... | collective-permute-start | bytes 196616 | tf_op jit(solution)/shard_map/ppermute | solution.py:427
  11.4 3.1 %collective-permute-start.2 = (bf16[256,128]{1,0:T(8,128)(2,1)S(1)}, bf16[256,128]{1,0:T(8,128)(2,1)S(1)}, u32[]{:S(2)}, u32[]{:S(2)}) collective-permute-start(bf16[256,128]{1,0:T(8,128)(2,1)S(1)} %get-tuple-element.22), channel_id=1, source_target_pairs={{0,1},{1,0},{2,3},{3,2},{4,5},{5,4},{6,7},{7,6},{8,9},{9,8},{10,11... | collective-permute-start | bytes 196616 | tf_op jit(solution)/shard_map/ppermute | solution.py:427
  14.5 28.2 %copy-start = (f32[48,32]{1,0:T(8,128)S(1)}, f32[48,32]{1,0:T(8,128)}, u32[]{:S(2)}) copy-start(f32[48,32]{1,0:T(8,128)} %constant.23.clone.table_ref) | copy-start | bytes 18436

commit v6 on v5

--- a/solution.py
+++ b/solution.py
@@ -152,8 +152,7 @@
     left = dst // lanes * 2
     pick_ref[...] = as_bf16(((at == 0) & (src == left)) | ((at == lanes - 1) & (src == left + 1)))
 
-    @pl.loop(0, levels)
-    def _(l):
+    for l in range(levels):
         for h in range(2):
             for c in range(comps):
                 for g in range(thirds):
@@ -377,8 +376,7 @@
         full = jnp.dot(tall, widen, preferred_element_type=F32)
         mix_ref[:, k * deep : (k + 1) * deep] = jnp.where(same, full, 0.0).astype(BF16)
 
-    @pl.loop(0, levels)
-    def _(l):
+    for l in range(levels):
         for s in range(kinds):
             for g in range(0, groups, 2):
                 x = jnp.concatenate([f_ref[l, s, g], f_ref[l, s, g + 1]], axis=1)

time: 49.7 us -> 49.3 us (level)
  Pallas kernels: 15.4 us -> 14.8 us
where the time goes in v6:
time: 49.3 us; the launch traced here: 49.2 us
  blocking collectives  25.4 us (52%)
  Pallas kernels  14.8 us (30%)
  starting transfers between devices  7.62 us (15%)
  waiting for transfers between devices  1.21 us (2%)
    all_to_all x2, blocking collectives, exchange(): return lax.all_to_all(copies, axes, split_axis=0, concat_axis=0, tiled=True)  25.4 us
    ppermute x4, starting transfers between devices, swap(): return lax.ppermute(x, axes, pairs)  7.62 us
    pallas_call x1, Pallas kernels, basis_of(): pl.pallas_call(functools.partial(basis_kernel, total_rows), in_specs=[who...  6.42 us
    pallas_call x1, Pallas kernels, pack(): pl.pallas_call(pack_kernel, in_specs=[pl.BlockSpec(memory_space=pltpu.HBM...  2.9 us
    pallas_call x1, Pallas kernels, outer(): pl.pallas_call(functools.partial(outer_kernel, step_lon, step_lat), in_sp...  2.74 us
    pallas_call x1, Pallas kernels, inner(): pl.pallas_call(functools.partial(inner_kernel, step_lon, step_lat), in_sp...  2.72 us
    ppermute x4, waiting for transfers between devices, swap(): return lax.ppermute(x, axes, pairs)  1.21 us
  transfers between devices with their start and end apart: 4, of which 2 were waited for; matrix products, arithmetic and copies ran while one was open for 0% of the time, Pallas kernels for 6%

profile of v6, /device:TPU:1, one launch (start us, length us, event | category | flops | bytes accessed | tf_op | source)
XLA Modules:
  0.0 49.2 jit_solution(6836784308881917906)
XLA Ops:
  0.0 2.9 %pack.1 = (bf16[256,128]{1,0:T(8,128)(2,1)S(1)}, bf16[256,128]{1,0:T(8,128)(2,1)S(1)}, bf16[256,128]{1,0:T(8,128)(2,1)S(1)}, bf16[2,32,4,48,128]{4,3,2,1,0:T(8,128)(2,1)S(1)}) custom-call(bf16[2,32,4,48,128]{4,3,2,1,0:T(8,128)(2,1)} %w_hbm.1), custom_call_target="tpu_custom_call" | custom-call | tf_op jit(solution)/shard_map/pack/pallas_call | solution.py:112
  2.9 3.3 %collective-permute-start = (bf16[256,128]{1,0:T(8,128)(2,1)S(1)}, bf16[256,128]{1,0:T(8,128)(2,1)S(1)}, u32[]{:S(2)}, u32[]{:S(2)}) collective-permute-start(bf16[256,128]{1,0:T(8,128)(2,1)S(1)} %get-tuple-element.19), channel_id=1, source_target_pairs={{0,8},{8,0},{1,9},{9,1},{2,10},{10,2},{3,11},{11,3},{4,12},{12,4},... | collective-permute-start | bytes 196616 | tf_op jit(solution)/shard_map/ppermute | solution.py:425
  6.2 0.0 collective-permute-start.1
  6.2 0.1 cosine_select_fusion.cos_ref
  6.3 0.8 %collective-permute-done.near_ref = bf16[256,128]{1,0:T(8,128)(2,1)S(1)} collective-permute-done((bf16[256,128]{1,0:T(8,128)(2,1)S(1)}, bf16[256,128]{1,0:T(8,128)(2,1)S(1)}, u32[]{:S(2)}, u32[]{:S(2)}) %collective-permute-start) | collective-permute-done | bytes 65568 | tf_op jit(solution)/shard_map/ppermute | solution.py:425
  7.1 4.3 %collective-permute-start.3 = (bf16[256,128]{1,0:T(8,128)(2,1)S(1)}, bf16[256,128]{1,0:T(8,128)(2,1)S(1)}, u32[]{:S(2)}, u32[]{:S(2)}) collective-permute-start(bf16[256,128]{1,0:T(8,128)(2,1)S(1)} %get-tuple-element.22), channel_id=1, source_target_pairs={{1,2},{2,1},{3,4},{4,3},{5,6},{6,5},{7,0},{0,7},{9,10},{10,9},{11,... | collective-permute-start | bytes 196616 | tf_op jit(solution)/shard_map/ppermute | solution.py:425
  11.4 0.0 collective-permute-start.2
  11.4 2.7 %inner.1 = (f32[4,2,6,256,128]{4,3,2,1,0:T(8,128)S(1)}, bf16[128,1536]{1,0:T(8,128)(2,1)S(1)}) custom-call(bf16[2,32,4,48,128]{4,3,2,1,0:T(8,128)(2,1)S(1)} %get-tuple-element.15.w_ref, f32[8,128]{1,0:T(8,128)S(1)} %cosine_select_fusion.cos_ref), custom_call_target="tpu_custom_call" | custom-call | flops 805306368 | bytes 9437184 | tf_op jit(solution)/shard_map/inner/pallas_call | solution.py:191
  14.2 0.0 collective-permute-done.1.far_ref
  14.2 0.0 collective-permute-done.3.sideb_ref
  14.2 0.4 collective-permute-done.2.sidea_ref
  14.5 0.0 copy-start
  14.5 2.7 %outer.1 = (bf16[4,2,6,256,128]{4,3,2,1,0:T(8,128)(2,1)S(1)}, f32[8,128]{1,0:T(8,128)S(1)}) custom-call(f32[4,2,6,256,128]{4,3,2,1,0:T(8,128)S(1)} %get-tuple-element.16.g_ref, bf16[128,1536]{1,0:T(8,128)(2,1)S(1)} %get-tuple-element.17.pick_ref, bf16[256,128]{1,0:T(8,128)(2,1)S(1)} %collective-permute-done.near_ref, ...), custom_call_target="tpu_custom_call" | custom-call | tf_op jit(solution)/shard_map/outer/pallas_call | solution.py:290
  17.3 16.4 %all_to_all.10 = f32[16,8,128]{2,1,0:T(8,128)S(1)} all-to-all(f32[16,8,128]{2,1,0:T(8,128)S(1)} %broadcast_in_dim.11), channel_id=1, replica_groups=mesh['lon_0'=4,'lon_1'=4,'lon_2'=2,'lat'=8] {'lon_2','lat'}, dimensions={0} | all-to-all | bytes 131072 | tf_op jit(solution)/shard_map/all_to_all | solution.py:417
  33.7 9.1 %all_to_all.11.sums_ref = f32[16,8,128]{2,1,0:T(8,128)S(1)} all-to-all(f32[16,8,128]{2,1,0:T(8,128)S(1)} %broadcast_in_dim.12), channel_id=1, replica_groups=mesh['lon_0'=4,'lon_1'=4,'lon_2'=2,'lat'=8] {'lon_0','lon_1'}, dimensions={0} | all-to-all | bytes 131072 | tf_op jit(solution)/shard_map/all_to_all | solution.py:417
  42.8 0.0 copy-done
  42.8 6.4 %basis.1 = f32[48,2,4,48,128]{4,3,2,1,0:T(8,128)} custom-call(f32[16,8,128]{2,1,0:T(8,128)S(1)} %all_to_all.11.sums_ref, f32[48,32]{1,0:T(8,128)S(1)} %copy-done, bf16[4,2,6,256,128]{4,3,2,1,0:T(8,128)(2,1)S(1)} %get-tuple-element.24.f_ref), custom_call_target="tpu_custom_call" | custom-call | tf_op jit(solution)/shard_map/basis/pallas_call | solution.py:400
  (4 shorter events, 0.0 us)
Async XLA Ops:
  2.9 4.2 %collective-permute-start = (bf16[256,128]{1,0:T(8,128)(2,1)S(1)}, bf16[256,128]{1,0:T(8,128)(2,1)S(1)}, u32[]{:S(2)}, u32[]{:S(2)}) collective-permute-start(bf16[256,128]{1,0:T(8,128)(2,1)S(1)} %get-tuple-element.19), channel_id=1, source_target_pairs={{0,8},{8,0},{1,9},{9,1},{2,10},{10,2},{3,11},{11,3},{4,12},{12,4},... | collective-permute-start | bytes 196616 | tf_op jit(solution)/shard_map/ppermute | solution.py:425
  6.2 7.9 %collective-permute-start.1 = (bf16[256,128]{1,0:T(8,128)(2,1)S(1)}, bf16[256,128]{1,0:T(8,128)(2,1)S(1)}, u32[]{:S(2)}, u32[]{:S(2)}) collective-permute-start(bf16[256,128]{1,0:T(8,128)(2,1)S(1)} %get-tuple-element.21), channel_id=1, source_target_pairs={{8,16},{16,8},{24,32},{32,24},{40,48},{48,40},{56,64},{64,56},{72,... | collective-permute-start | bytes 196616 | tf_op jit(solution)/shard_map/ppermute | solution.py:425
  7.1 7.0 %collective-permute-start.3 = (bf16[256,128]{1,0:T(8,128)(2,1)S(1)}, bf16[256,128]{1,0:T(8,128)(2,1)S(1)}, u32[]{:S(2)}, u32[]{:S(2)}) collective-permute-start(bf16[256,128]{1,0:T(8,128)(2,1)S(1)} %get-tuple-element.22), channel_id=1, source_target_pairs={{1,2},{2,1},{3,4},{4,3},{5,6},{6,5},{7,0},{0,7},{9,10},{10,9},{11,... | collective-permute-start | bytes 196616 | tf_op jit(solution)/shard_map/ppermute | solution.py:425
  11.4 3.1 %collective-permute-start.2 = (bf16[256,128]{1,0:T(8,128)(2,1)S(1)}, bf16[256,128]{1,0:T(8,128)(2,1)S(1)}, u32[]{:S(2)}, u32[]{:S(2)}) collective-permute-start(bf16[256,128]{1,0:T(8,128)(2,1)S(1)} %get-tuple-element.22), channel_id=1, source_target_pairs={{0,1},{1,0},{2,3},{3,2},{4,5},{5,4},{6,7},{7,6},{8,9},{9,8},{10,11... | collective-permute-start | bytes 196616 | tf_op jit(solution)/shard_map/ppermute | solution.py:425
  14.5 28.2 %copy-start = (f32[48,32]{1,0:T(8,128)S(1)}, f32[48,32]{1,0:T(8,128)}, u32[]{:S(2)}) copy-start(f32[48,32]{1,0:T(8,128)} %constant.23.clone.table_ref) | copy-start | bytes 18436
